TPU v7x, 128 devices: a whole 4x4x4 slice. The times are simulated.
128 devices in a mesh: tgt: 16 (over z, x), src: 8 (over y, core).
Axes of the slice: x: 4, y: 4, z: 4, core: 2. Of those that a mesh axis runs over, the one named last changes fastest.
Arguments:
- points: bfloat16 [262144, 256], P(('tgt', 'src')), may hold values from -0.4 to 0.4
- weights: bfloat16 [262144, 64], P(('tgt', 'src')), may hold values from -6 to 6
- near_list: int32 [2048, 16], P(('tgt', 'src')), may hold values from -1 to 127, as said below
- far_list: int32 [2048, 3, 8], P('tgt', None, 'src'), may hold values from -1 to 63, as said below
- skel_index: int32 [896, 256], P(('tgt', 'src')), may hold values from 0 to 2047, as said below
- equiv_weights: bfloat16 [896, 256, 64], P(('tgt', 'src')), may hold values from -6 to 6
Outputs:
- potential: float32 [262144, 64], P(('tgt', 'src'))
Inputs may be any that keep to these rules, and one draw needn't show every extreme that they name: `near_list`: row b lists blocks of b's group of 128 blocks by their index within the group: first b itself, then distinct other blocks; after a row's live entries all are -1; every row has 4 or more live entries. `far_list`: entry [b, l, c] is -1 or a level-l node owned by a device of src index c, numbered as the owner's tgt index times (16 // (4 * 2 ** l)) plus the node's number among the owner's level-l nodes. `skel_index`: Level-l nodes of a device cover 4 * 128 * 2 ** l consecutive points of that device each, in order; a node's 256 entries are increasing indices of the device's points inside the node.
All inputs are finite; a program needn't handle non-finite values.
Results may differ from a plain program's by a relative error of at most 0.0023.
Values may be sent and summed in bfloat16 or wider, within the bound.
No kernel may reach another device: no remote copies, remote signals or barrier semaphores. Data moves between devices by JAX's collectives and lax.ppermute only.
A program may use at most 192 MiB of HBM per device.

v0:
```python
import jax
import jax.numpy as jnp
from jax import lax
from jax.experimental import pallas as pl
from jax.experimental.pallas import tpu as pltpu
from jax.sharding import PartitionSpec as P

E = 256
WCOL = 64
BLK = 128
RANK = 256
NEAR = 16
LEVELS = 3
BLK_DEV = 16
NODE_DEV = 7
PTS = BLK_DEV * BLK
WROWS = BLK_DEV * 32 + 32
PACK = PTS + WROWS
NODE = RANK + WCOL
DATA = NODE_DEV * NODE // 2
HALF = DATA + 16
BLOCKS = 8 * BLK_DEV
LOG2E = 1.4426950408889634
DOT_SCALE = 4.0 * LOG2E
NORM_SCALE = 2.0 * LOG2E
DEAD = 1e30
GROUP = 4
SLACK = 3 * GROUP
F32 = jnp.float32
BF16 = jnp.bfloat16
NT = (((1,), (1,)), ((), ()))


def row_norms(x):
    v = x.astype(F32)
    sq = v * v
    half = sq[:, 0:128] + sq[:, 128:256]
    parts = [jnp.sum(half[i : i + 128].T, axis=0, keepdims=True) for i in range(0, x.shape[0], 128)]
    row = parts[0] if len(parts) == 1 else jnp.concatenate(parts, axis=1)
    return row * NORM_SCALE


def column_of(row, copies=2):
    col = jnp.broadcast_to(row, (128, 128)).T
    return jnp.concatenate([col] * copies, axis=1)


def relative(there, here):
    d = (there - here) & 3
    return jnp.where(d == 0, 0, jnp.where(d == 3, 1, d + 1))


def three_parts(v):
    hi = v.astype(BF16).astype(F32)
    mid = (v - hi).astype(BF16).astype(F32)
    return hi, mid, v - hi - mid


def prep_body(pts, wts, ewts, idx, y_out, half_a, half_b, norms):
    def node(r, first, size):
        parts = []
        for c in range(0, RANK, 128):
            want = column_of(idx[r : r + 1, c : c + 128].astype(F32), size // 128)
            iota = lax.broadcasted_iota(jnp.int32, (128, size), 1).astype(F32)
            pick = jnp.where(iota == want - first, 1.0, 0.0).astype(BF16)
            rows = lax.dot_general(
                pick, pts[first : first + size, :], (((1,), (0,)), ((), ())), preferred_element_type=F32
            )
            parts.append(rows.astype(BF16))
        rows = jnp.concatenate(parts, axis=0)
        for c, part in enumerate(three_parts(row_norms(rows))):
            row = (16 if r >= 3 else 0) + c * 4 + (r - 3 if r >= 3 else r)
            norms[row : row + 1, :] = part
        return rows

    norms[...] = jnp.zeros((32, E), F32)
    cut = DATA - 3 * NODE
    for r in range(3):
        half_a[r * NODE : r * NODE + RANK, :] = node(r, r * 512, 512)
        half_a[r * NODE + RANK : (r + 1) * NODE, :] = ewts[r]
    rows = node(3, 3 * 512, 512)
    half_a[3 * NODE : DATA, :] = rows[0:cut]
    half_b[0 : RANK - cut, :] = rows[cut:RANK]
    half_b[RANK - cut : NODE - cut, :] = ewts[3]
    for r, first, size in ((4, 0, 1024), (5, 1024, 1024), (6, 0, 2048)):
        row = r * NODE - DATA
        half_b[row : row + RANK, :] = node(r, first, size)
        half_b[row + RANK : row + NODE, :] = ewts[r]
    half_a[DATA:HALF, :] = norms[0:16, :].astype(BF16)
    half_b[DATA:HALF, :] = norms[16:32, :].astype(BF16)
    y_out[0:PTS, :] = pts[...]
    for b in range(BLK_DEV):
        w = wts[:, b * BLK : (b + 1) * BLK]
        row = PTS + b * 32
        y_out[row : row + 32, 0:BLK] = w[0:32]
        y_out[row : row + 32, BLK:E] = w[32:64]
        for c, part in enumerate(three_parts(row_norms(pts[b * BLK : (b + 1) * BLK, :]))):
            at = b + c // 2 * 16
            norms[at : at + 1, c % 2 * BLK : (c % 2 + 1) * BLK] = part
    norms[16:32, BLK:E] = jnp.zeros((16, BLK), F32)
    y_out[PACK - 32 : PACK, :] = norms[...].astype(BF16)


def prep(points, weights_t, equiv_t, skel_index):
    return pl.pallas_call(
        prep_body,
        out_shape=(
            jax.ShapeDtypeStruct((PACK, E), BF16),
            jax.ShapeDtypeStruct((HALF, E), BF16),
            jax.ShapeDtypeStruct((HALF, E), BF16),
        ),
        scratch_shapes=[pltpu.VMEM((32, E), F32)],
        cost_estimate=pl.CostEstimate(flops=10**9, bytes_accessed=8 * 10**6, transcendentals=0),
        name="prep",
    )(points, weights_t, equiv_t, skel_index)


def run_entries(total, dots, finish, s0, s1, before=None, state=0):
    def pair(j, state):
        first = j * 2 * GROUP
        if before is not None:
            state = before(j, state)
        dots(first + GROUP, s1)
        finish(first, s0)
        dots(first + 2 * GROUP, s0)
        finish(first + GROUP, s1)
        return state

    dots(0, s0)
    return lax.fori_loop(0, (total + 2 * GROUP - 1) // (2 * GROUP), pair, state)


def sorted_entries(far, tgt_index, src_index):
    level = lax.broadcasted_iota(jnp.int32, far.shape, 0)
    b = lax.broadcasted_iota(jnp.int32, far.shape, 1)
    src = b // BLK_DEV
    slot = ((src & 1) ^ (src_index & 1)) * 4 + relative(src // 2, src_index // 2)
    w = jnp.maximum(far, 0)
    owner = w >> (2 - level)
    r = (w & ((4 >> level) - 1)) + jnp.where(level == 0, 0, 2 * level + 2)
    i, j = relative(owner // 4, tgt_index // 4), relative(owner & 3, tgt_index & 3)
    of_i, of_j = jnp.where(i == 3, 2, jnp.minimum(i, 1)), jnp.where(j == 3, 2, jnp.minimum(j, 1))
    cls = jnp.where(r < 3, of_j, jnp.where(r > 3, of_i, jnp.maximum(of_i, of_j)))
    order = [0] * (16 * NODE_DEV)
    for group in range(3):
        for n, (i2, j2, r2) in enumerate(class_nodes(group)):
            order[(i2 * 4 + j2) * NODE_DEV + r2] = n
    place = (i * 4 + j) * NODE_DEV + r
    hit = place[..., None] == jnp.arange(len(order), dtype=jnp.int32)
    node = jnp.sum(jnp.where(hit, jnp.array(order, jnp.int32), 0), axis=-1)
    node = jnp.where(far >= 0, node, level)
    cls = jnp.where(far >= 0, cls, 3).reshape(-1)
    keys = (cls << 14) | ((slot * BLK_DEV + b % BLK_DEV) << 7 | node).reshape(-1)
    rank = jnp.sum((keys[None, :] < keys[:, None]).astype(jnp.int32), axis=1)
    places = jnp.arange(keys.shape[0], dtype=jnp.int32)
    entries = jnp.sum(jnp.where(rank[None, :] == places[:, None], keys[None, :], 0), axis=1)
    starts = jnp.sum((cls[None, :] < jnp.arange(4, dtype=jnp.int32)[:, None]).astype(jnp.int32), axis=1)
    return entries, starts


def class_nodes(group):
    cls = (0, 1, 1, 2)
    grid = [(i, j) for i in range(4) for j in range(4)]
    nodes = [(i, j, r) for i, j in grid if cls[j] == group for r in range(3)]
    nodes += [(i, j, r) for i, j in grid if cls[i] == group for r in range(4, NODE_DEV)]
    return nodes + [(i, j, 3) for i, j in grid if max(cls[i], cls[j]) == group]


def panel_nodes(group):
    return (len(class_nodes(group)) + 3) // 4 * 4


def panel_layout(group):
    cut = DATA - 3 * NODE
    rows, norms = [], []
    for n, (i, j, r) in enumerate(class_nodes(group)):
        if r == 0:
            spans = [(0, 0, 3 * NODE, 0)]
        elif r == 3:
            spans = [(0, DATA - cut, cut, 0), (1, 0, NODE - cut, cut)]
        elif r == 4:
            spans = [(1, NODE - cut, 3 * NODE, 0)]
        else:
            continue
        for half, row, count, place in spans:
            first, second = (i, j) if half == 0 else (j, i)
            rows.append((half, second * 2 + first // 2, (first % 2) * HALF + row, count, n * NODE + place))
        norms.append((half, second * 2 + first // 2, (first % 2) * HALF + DATA, 16, len(norms) * 16))
    return rows, norms


def panel_norms(group, parts, wide, node_norms):
    wide[...] = parts[...].astype(F32)
    k = -1
    for n, (i, j, r) in enumerate(class_nodes(group)):
        if r in (0, 3, 4):
            k += 1
        row = k * 16 + (r if r < 3 else r - 3)
        node_norms[n : n + 1, :] = wide[row : row + 1, :] + wide[row + 4 : row + 5, :] + wide[row + 8 : row + 9, :]


def run_far(group, starts, entries, xs, norm_ref, pan, node_norms, out_v, s0, s1, arrive=None):
    start, end = starts[group], starts[group + 1]

    def entry(e):
        live = start + e < end
        code = entries[jnp.minimum(start + e, BLOCKS * LEVELS - 1)]
        b = jnp.where(live, (code >> 7) & 127, BLOCKS)
        return b, jnp.where(live, code & 127, 0)

    def dots(first, s_ref):
        for u in range(GROUP):
            b, n = entry(first + u)
            b = jnp.minimum(b, BLOCKS - 1)
            x = xs[pl.ds(pl.multiple_of(b * BLK, BLK), BLK), :]
            src = pan[pl.ds(pl.multiple_of(n * NODE, NODE), RANK), :]
            dot = lax.dot_general(x, src, NT, preferred_element_type=F32)
            s_ref[u] = dot * DOT_SCALE - column_of(norm_ref[pl.ds(b, 1), :])

    def finish(first, s_ref):
        for u in range(GROUP):
            b, n = entry(first + u)
            k = jnp.exp2(s_ref[u] - node_norms[pl.ds(n, 1), :]).astype(BF16)
            wt = pan[pl.ds(pl.multiple_of(n * NODE, NODE) + RANK, WCOL), :]
            out_v[b] = out_v[b] + lax.dot_general(wt, k, NT, preferred_element_type=F32)

    if arrive is None:
        run_entries(end - start, dots, finish, s0, s1)
        return

    def needed(e):
        return jnp.minimum(entry(e)[0] // BLK_DEV, 7) + 1

    arrived = arrive(0, needed(GROUP - 1))

    def before(j, arrived):
        return arrive(arrived, needed(j * 2 * GROUP + 3 * GROUP - 1))

    arrived = run_entries(end - start, dots, finish, s0, s1, before, arrived)
    arrive(arrived, 8)


def near_call(meta, near_list, starts, entries, pieces, panels, rows, nrows):
    count = len(panels)

    def body(meta, near, starts, entries, *refs):
        pieces, sources, refs = refs[:10], refs[10 : 10 + count], refs[10 + count :]
        x_out, norm_out, near_out, sums_out, *refs = refs
        xs, ws, pan, parts, wide, node_norms, acc, out_v, s0, s1, targets, slots, sems, wsem, psem, out_sems = refs
        y, core = meta[1] // 2, meta[1] & 1

        def store(k):
            return pltpu.make_async_copy(xs.at[pl.ds(k * PTS, PTS), :], x_out.at[k], out_sems.at[k])

        loads, cut = [], PACK // 2
        for k in range(8):
            p = k // 4 * 5 + k % 4
            spans = [(p, 0, PTS)] if k % 4 < 3 else [(p, 0, cut), (p + 1, cut, PTS - cut)]
            for piece, row, size in spans:
                first = 0 if piece != p + 1 else row - cut
                loads.append(
                    pltpu.make_async_copy(
                        pieces[piece].at[pl.ds(first, size), :], xs.at[pl.ds(k * PTS + row, size), :], sems.at[piece]
                    )
                )
            piece, first = (p, PTS) if k % 4 < 3 else (p + 1, PTS - cut)
            loads.append(
                pltpu.make_async_copy(
                    pieces[piece].at[pl.ds(first, WROWS), :], ws.at[pl.ds(k * WROWS, WROWS), :], wsem.at[k]
                )
            )

        panel_copies = [
            pltpu.make_async_copy(sources[p].at[pl.ds(a, r), :], to.at[pl.ds(d, r), :], psem.at[i])
            for i, (to, p, a, r, d) in enumerate([(pan, *item) for item in rows] + [(parts, *item) for item in nrows])
        ]
        for copy in loads:
            copy.start()

        def scan_near(i, n):
            for p in range(NEAR // 2):
                targets[n] = i
                slots[n] = 2 * p
                n = n + jnp.where(near[i, 2 * p] >= 0, 1, 0)
            acc[i] = jnp.zeros((WCOL, BLK), F32)
            return n

        total = lax.fori_loop(0, BLK_DEV, scan_near, 0)
        for i in range(SLACK):
            targets[total + i] = BLK_DEV
            slots[total + i] = 0
        acc[BLK_DEV] = jnp.zeros((WCOL, BLK), F32)

        def clear(b, carry):
            out_v[b] = jnp.zeros((WCOL, BLK), F32)
            return carry

        lax.fori_loop(0, BLOCKS + 1, clear, 0)
        for k in range(8):
            for copy in (loads[k // 4 * 9 + k % 4 * 2 :])[: 3 if k % 4 == 3 else 2]:
                copy.wait()
            store(k).start()

            v = ws[pl.ds(k * WROWS + WROWS - 32, 32), :].astype(F32)
            norm_out[pl.ds(k * BLK_DEV, BLK_DEV), :] = v[0:16, 0:BLK] + v[0:16, BLK:E] + v[16:32, 0:BLK]
        for copy in panel_copies:
            copy.start()

        def source(i, slot):
            v = near[i, slot]
            j = jnp.maximum(v, 0)
            k = (((j // BLK_DEV) & 1) ^ core) * 4 + relative(j // (2 * BLK_DEV), y)
            return v, k, j % BLK_DEV

        def dots(first, s_ref):
            for u in range(GROUP):
                i = jnp.minimum(targets[first + u], BLK_DEV - 1)
                x = xs[pl.ds(pl.multiple_of(i * BLK, BLK), BLK), :]
                srcs, rows = [], []
                for s in range(2):
                    v, k, b = source(i, slots[first + u] + s)
                    srcs.append(xs[pl.ds(pl.multiple_of(k * PTS + b * BLK, BLK), BLK), :])
                    bias = jnp.where(v >= 0, 0.0, DEAD).astype(F32)
                    rows.append(norm_out[pl.ds(k * BLK_DEV + b, 1), :] + bias)
                dot = lax.dot_general(x, jnp.concatenate(srcs, axis=0), NT, preferred_element_type=F32)
                col = column_of(norm_out[pl.ds(i, 1), :])
                s_ref[u] = dot * DOT_SCALE - col - jnp.concatenate(rows, axis=1)

        def finish(first, s_ref):
            for u in range(GROUP):
                target = targets[first + u]
                i = jnp.minimum(target, BLK_DEV - 1)
                wts = []
                for s in range(2):
                    _, k, b = source(i, slots[first + u] + s)
                    w = ws[pl.ds(pl.multiple_of(k * WROWS + b * 32, 32), 32), :]
                    wts.append(jnp.concatenate([w[:, 0:128], w[:, 128:256]], axis=0))
                k = jnp.exp2(s_ref[u]).astype(BF16)
                acc[target] = acc[target] + lax.dot_general(
                    jnp.concatenate(wts, axis=1), k, NT, preferred_element_type=F32
                )

        run_entries(total, dots, finish, s0, s1)
        near_out[...] = acc[0:BLK_DEV]

        for copy in panel_copies:
            copy.wait()
        panel_norms(0, parts, wide, node_norms)

        run_far(0, starts, entries, xs, norm_out, pan, node_norms, out_v, s0, s1)
        result = pltpu.make_async_copy(out_v.at[pl.ds(0, BLOCKS)], sums_out, out_sems.at[8])
        result.start()
        for k in range(8):
            store(k).wait()
        result.wait()

    anys = pl.BlockSpec(memory_space=pl.ANY)
    vm = pl.BlockSpec(memory_space=pltpu.VMEM)
    return pl.pallas_call(
        body,
        grid_spec=pltpu.PrefetchScalarGridSpec(
            num_scalar_prefetch=4,
            grid=(),
            in_specs=[anys] * (10 + count),
            out_specs=[anys, vm, vm, anys],
            scratch_shapes=[
                pltpu.VMEM((8 * PTS, E), BF16),
                pltpu.VMEM((8 * WROWS, E), BF16),
                pltpu.VMEM((panel_nodes(0) * NODE, E), BF16),
                pltpu.VMEM((len(nrows) * 16, E), BF16),
                pltpu.VMEM((len(nrows) * 16, E), F32),
                pltpu.VMEM((panel_nodes(0), RANK), F32),
                pltpu.VMEM((BLK_DEV + 1, WCOL, BLK), F32),
                pltpu.VMEM((BLOCKS + 1, WCOL, BLK), F32),
                pltpu.VMEM((GROUP, BLK, RANK), F32),
                pltpu.VMEM((GROUP, BLK, RANK), F32),
                pltpu.SMEM((BLK_DEV * NEAR // 2 + SLACK,), jnp.int32),
                pltpu.SMEM((BLK_DEV * NEAR // 2 + SLACK,), jnp.int32),
                pltpu.SemaphoreType.DMA((10,)),
                pltpu.SemaphoreType.DMA((8,)),
                pltpu.SemaphoreType.DMA((len(rows) + len(nrows),)),
                pltpu.SemaphoreType.DMA((9,)),
            ],
        ),
        out_shape=[
            jax.ShapeDtypeStruct((8, PTS, E), BF16),
            jax.ShapeDtypeStruct((BLOCKS, BLK), F32),
            jax.ShapeDtypeStruct((BLK_DEV, WCOL, BLK), F32),
            jax.ShapeDtypeStruct((BLOCKS, WCOL, BLK), F32),
        ],
        cost_estimate=pl.CostEstimate(flops=9 * 10**9, bytes_accessed=30 * 10**6, transcendentals=6 * 10**6),
        name="near",
    )(meta, near_list, starts, entries, *pieces, *panels)


def far_call(group, starts, entries, x_all, norms, accs, panels, rows, nrows):
    count, extra = len(panels), len(accs)
    last = extra > 0

    def body(starts, entries, x_hbm, norm_ref, *refs):
        sources, sums, refs = refs[:count], refs[count : count + extra], refs[count + extra :]
        if last:
            keep_hbm, send_hbm, *refs, acc_v, send_v = refs
        else:
            out_hbm, *refs = refs
        out_v, xs, pan, parts, wide, node_norms, s0, s1, psem, xsem, osem = refs
        panel_copies = [
            pltpu.make_async_copy(sources[p].at[pl.ds(a, r), :], to.at[pl.ds(d, r), :], psem.at[i])
            for i, (to, p, a, r, d) in enumerate([(pan, *item) for item in rows] + [(parts, *item) for item in nrows])
        ]
        acc_copies = [pltpu.make_async_copy(sums[i], acc_v.at[i], osem.at[i]) for i in range(extra)]

        def x_copy(k):
            return pltpu.make_async_copy(x_hbm.at[k], xs.at[pl.ds(k * PTS, PTS), :], xsem.at[k])

        for copy in panel_copies + [x_copy(k) for k in range(8)] + acc_copies:
            copy.start()

        def clear(b, carry):
            out_v[b] = jnp.zeros((WCOL, BLK), F32)
            return carry

        lax.fori_loop(0, BLOCKS + 1, clear, 0)
        for copy in panel_copies:
            copy.wait()
        panel_norms(group, parts, wide, node_norms)

        def arrive(done, upto):
            def wait(k, carry):
                x_copy(k).wait()
                return carry

            lax.fori_loop(done, upto, wait, 0)
            return jnp.maximum(done, upto)

        run_far(group, starts, entries, xs, norm_ref, pan, node_norms, out_v, s0, s1, arrive)
        if last:
            for copy in acc_copies:
                copy.wait()

            def merge(b, carry):
                c = BLOCKS // 2 + b
                send_v[b] = (out_v[c] + (acc_v[0, c] + acc_v[1, c])).astype(BF16)
                return carry

            def merge_kept(b, carry):
                out_v[b] = out_v[b] + (acc_v[0, b] + acc_v[1, b])
                return carry

            copies = [
                pltpu.make_async_copy(send_v, send_hbm, osem.at[0]),
                pltpu.make_async_copy(out_v.at[pl.ds(0, BLOCKS // 2)], keep_hbm, osem.at[1]),
            ]
            lax.fori_loop(0, BLOCKS // 2, merge, 0)
            copies[0].start()
            lax.fori_loop(0, BLOCKS // 2, merge_kept, 0)
            copies[1].start()
        else:
            copies = [pltpu.make_async_copy(out_v.at[pl.ds(0, BLOCKS)], out_hbm, osem.at[0])]
            copies[0].start()
        for copy in copies:
            copy.wait()

    anys = pl.BlockSpec(memory_space=pl.ANY)
    sums = (BLOCKS, WCOL, BLK)
    half = (BLOCKS // 2, WCOL, BLK)
    return pl.pallas_call(
        body,
        grid_spec=pltpu.PrefetchScalarGridSpec(
            num_scalar_prefetch=2,
            grid=(),
            in_specs=[anys, pl.BlockSpec(memory_space=pltpu.VMEM)] + [anys] * (count + extra),
            out_specs=(anys, anys) if last else anys,
            scratch_shapes=[
                pltpu.VMEM((BLOCKS + 1, WCOL, BLK), F32),
                pltpu.VMEM((8 * PTS, E), BF16),
                pltpu.VMEM((panel_nodes(group) * NODE, E), BF16),
                pltpu.VMEM((len(nrows) * 16, E), BF16),
                pltpu.VMEM((len(nrows) * 16, E), F32),
                pltpu.VMEM((panel_nodes(group), RANK), F32),
                pltpu.VMEM((GROUP, BLK, RANK), F32),
                pltpu.VMEM((GROUP, BLK, RANK), F32),
                pltpu.SemaphoreType.DMA((len(rows) + len(nrows),)),
                pltpu.SemaphoreType.DMA((8,)),
                pltpu.SemaphoreType.DMA((2,)),
            ]
            + ([pltpu.VMEM((extra, *sums), F32), pltpu.VMEM(half, BF16)] if last else []),
        ),
        out_shape=(jax.ShapeDtypeStruct(half, F32), jax.ShapeDtypeStruct(half, BF16))
        if last
        else jax.ShapeDtypeStruct(sums, F32),
        cost_estimate=pl.CostEstimate(
            flops=(5 if last else 10) * 10**9, bytes_accessed=25 * 10**6, transcendentals=6 * 10**6
        ),
    )(starts, entries, x_all, norms, *panels, *accs)


def shards(points, weights, near_list, far_list, skel_index, equiv_weights):
    def along_y(d):
        return [(s, ((s // 2 + d) % 4) * 2 + s % 2) for s in range(8)]

    def along_z(d):
        return [(t, ((t // 4 + d) % 4) * 4 + t % 4) for t in range(16)]

    def along_x(d):
        return [(t, (t // 4) * 4 + (t % 4 + d) % 4) for t in range(16)]

    partner = [(s, s ^ 1) for s in range(8)]

    def move(v, axis, pairs):
        return lax.ppermute(v, axis, pairs)

    meta = jnp.stack([lax.axis_index("tgt"), lax.axis_index("src")]).astype(jnp.int32)
    entries, starts = sorted_entries(far_list[:, :, 0].T, lax.axis_index("tgt"), lax.axis_index("src"))
    pack, half_a, half_b = prep(points, weights.T, jnp.swapaxes(equiv_weights, 1, 2), skel_index)

    def first_axis(v, along):
        return [v] + [move(v, "tgt", along(d)) for d in (1, -1, 2)]

    def second_axis(v, along):
        low, high = jnp.concatenate(v[:2], axis=0), jnp.concatenate(v[2:], axis=0)
        up0, down1 = move(low, "tgt", along(1)), move(high, "tgt", along(-1))
        up1, down0 = move(high, "tgt", along(1)), move(low, "tgt", along(-1))
        return [low, high, up0, up1, down0, down1, move(up0, "tgt", along(1)), move(down1, "tgt", along(-1))]

    a4 = first_axis(half_a, along_z)
    b4 = first_axis(half_b, along_x)
    panels = second_axis(a4, along_x) + second_axis(b4, along_z)
    up, down = move(pack, "src", along_y(1)), move(pack, "src", along_y(-1))
    cut = PACK // 2
    mine = [pack, up, down, move(up[:cut], "src", along_y(1)), move(down[cut:], "src", along_y(-1))]
    pieces = mine + [move(v, "src", partner) for v in mine]

    def operands(group):
        kinds = panel_layout(group)
        used = sorted({half * 8 + p for items in kinds for half, p, _, _, _ in items})
        copies = [[(used.index(h * 8 + p), a, r, d) for h, p, a, r, d in items] for items in kinds]
        return [panels[u] for u in used], *copies

    x_all, norms, near_sum, sums0 = near_call(meta, near_list, starts, entries, pieces, *operands(0))
    sums1 = far_call(1, starts, entries, x_all, norms, [], *operands(1))
    keep, send = far_call(2, starts, entries, x_all, norms, [sums0, sums1], *operands(2))

    half = (4, BLK_DEV, WCOL, BLK)
    keep, got = keep.reshape(half), move(send, "src", partner).reshape(half)
    out = near_sum + keep[0] + got[0].astype(F32)
    for i, d in ((3, 2), (1, -1), (2, 1)):
        chip = (keep[i] + got[i].astype(F32)).astype(BF16)
        out = out + move(chip, "src", along_y(d)).astype(F32)
    return out.transpose(0, 2, 1).reshape(PTS, WCOL)


def solution(mesh):
    in_specs = (
        P(("tgt", "src"), None),
        P(("tgt", "src"), None),
        P(("tgt", "src"), None),
        P("tgt", None, "src"),
        P(("tgt", "src"), None),
        P(("tgt", "src"), None, None),
    )
    out_specs = P(("tgt", "src"), None)

    return jax.shard_map(shards, mesh=mesh, in_specs=in_specs, out_specs=out_specs, check_vma=False)
```

profile of v0, /device:TPU:0, one launch (start us, length us, event | category | flops | bytes accessed | tf_op | source)
XLA Modules:
  0.0 218.6 jit_solution(17113271019481751920)
XLA Ops:
  0.0 4.0 %prep.1 = (bf16[2592,256]{1,0:T(8,128)(2,1)}, bf16[1136,256]{1,0:T(8,128)(2,1)}, bf16[1136,256]{1,0:T(8,128)(2,1)}) custom-call(bf16[2048,256]{1,0:T(8,128)(2,1)} %pts.1, bf16[64,2048]{1,0:T(8,128)(2,1)} %bitcast.88, bf16[7,64,256]{2,1,0:T(8,128)(2,1)} %bitcast.89, s32[7,256]{1,0:T(8,128)} %idx.1), custom_call_target="tpu_custom_call" | custom-call | flops 1000000000 | bytes 8000000 | tf_op jit(solution)/shard_map/prep/pallas_call | solution.py:105
  4.0 4.1 %collective-permute-start.10 = (bf16[1136,256]{1,0:T(8,128)(2,1)}, bf16[1136,256]{1,0:T(8,128)(2,1)S(1)}, u32[]{:S(2)}, u32[]{:S(2)}) collective-permute-start(bf16[1136,256]{1,0:T(8,128)(2,1)} %get-tuple-element.15), channel_id=1, source_target_pairs={{0,96},{8,104},{16,112},{24,120},{32,0},{40,8},{48,16},{56,24},{64... | collective-permute-start | bytes 1744904 | tf_op jit(solution)/shard_map/ppermute | solution.py:511
  8.2 2.8 %collective-permute-start.13 = (bf16[1136,256]{1,0:T(8,128)(2,1)}, bf16[1136,256]{1,0:T(8,128)(2,1)S(1)}, u32[]{:S(2)}, u32[]{:S(2)}) collective-permute-start(bf16[1136,256]{1,0:T(8,128)(2,1)} %get-tuple-element.16), channel_id=1, source_target_pairs={{0,24},{8,0},{16,8},{24,16},{32,56},{40,32},{48,40},{56,48},{64,88... | collective-permute-start | bytes 1744904 | tf_op jit(solution)/shard_map/ppermute | solution.py:511
  11.0 0.8 collective-permute-start.14
  11.8 1.3 collective-permute-start.9
  13.0 1.9 constant_dynamic-update-slice_fusion.1
  14.9 18.4 %collective-permute-done.10 = bf16[1136,256]{1,0:T(8,128)(2,1)S(1)} collective-permute-done((bf16[1136,256]{1,0:T(8,128)(2,1)}, bf16[1136,256]{1,0:T(8,128)(2,1)S(1)}, u32[]{:S(2)}, u32[]{:S(2)}) %collective-permute-start.10) | collective-permute-done | bytes 581664 | tf_op jit(solution)/shard_map/ppermute | solution.py:511
  33.4 1.6 collective-permute-start
  35.0 1.7 collective-permute-start.1
  36.8 2.8 %collective-permute-start.16 = (bf16[2272,256]{1,0:T(8,128)(2,1)S(1)}, bf16[2272,256]{1,0:T(8,128)(2,1)S(1)}, u32[]{:S(2)}, u32[]{:S(2)}) collective-permute-start(bf16[2272,256]{1,0:T(8,128)(2,1)S(1)} %constant_dynamic-update-slice_fusion.2.refs_11_.refs_1_.refs_0_), channel_id=1, source_target_pairs={{0,24},{8,0},{16,8},{24,16},{32,56},{40,32},{48,40},{56,48},{64,88... | collective-permute-start | bytes 3489800 | tf_op jit(solution)/shard_map/ppermute | solution.py:511
  39.7 0.9 constant_dynamic-update-slice_fusion.5
  40.6 0.9 constant_dynamic-update-slice_fusion.refs_10_.refs_0_
  41.5 15.5 %collective-permute-done.12 = bf16[1136,256]{1,0:T(8,128)(2,1)S(1)} collective-permute-done((bf16[1136,256]{1,0:T(8,128)(2,1)S(1)}, bf16[1136,256]{1,0:T(8,128)(2,1)S(1)}, u32[]{:S(2)}, u32[]{:S(2)}) %collective-permute-start.12) | collective-permute-done | bytes 581664 | tf_op jit(solution)/shard_map/ppermute | solution.py:511
  57.0 3.6 %collective-permute-start.21 = (bf16[2272,256]{1,0:T(8,128)(2,1)S(1)}, bf16[2272,256]{1,0:T(8,128)(2,1)}, u32[]{:S(2)}, u32[]{:S(2)}) collective-permute-start(bf16[2272,256]{1,0:T(8,128)(2,1)S(1)} %constant_dynamic-update-slice_fusion.6.refs_13_.refs_7_.refs_5_), channel_id=1, source_target_pairs={{0,96},{8,104},{16,112},{24,120},{32,0},{40,8},{48,16},{56,24},{64... | collective-permute-start | bytes 3489800 | tf_op jit(solution)/shard_map/ppermute | solution.py:511
  60.6 0.9 constant_dynamic-update-slice_fusion.4.refs_12_.refs_6_
  61.5 3.3 %collective-permute-done.refs_1_ = bf16[2592,256]{1,0:T(8,128)(2,1)S(1)} collective-permute-done((bf16[2592,256]{1,0:T(8,128)(2,1)}, bf16[2592,256]{1,0:T(8,128)(2,1)S(1)}, u32[]{:S(2)}, u32[]{:S(2)}) %collective-permute-start) | collective-permute-done | bytes 1327136 | tf_op jit(solution)/shard_map/ppermute | solution.py:511
  64.8 1.5 collective-permute-start.15
  66.4 1.6 collective-permute-start.17
  67.9 17.1 %collective-permute-done.21.refs_11_.refs_7_ = bf16[2272,256]{1,0:T(8,128)(2,1)} collective-permute-done((bf16[2272,256]{1,0:T(8,128)(2,1)S(1)}, bf16[2272,256]{1,0:T(8,128)(2,1)}, u32[]{:S(2)}, u32[]{:S(2)}) %collective-permute-start.21) | collective-permute-done | bytes 1163296 | tf_op jit(solution)/shard_map/ppermute | solution.py:511
  85.1 1.3 slice.48
  86.6 7.9 %collective-permute-done.15.refs_3_.refs_1_ = bf16[2272,256]{1,0:T(8,128)(2,1)} collective-permute-done((bf16[2272,256]{1,0:T(8,128)(2,1)S(1)}, bf16[2272,256]{1,0:T(8,128)(2,1)}, u32[]{:S(2)}, u32[]{:S(2)}) %collective-permute-start.15) | collective-permute-done | bytes 1163296 | tf_op jit(solution)/shard_map/ppermute | solution.py:511
  94.9 1.8 collective-permute-done.20.refs_9_.refs_6_
  96.6 1.7 collective-permute-start.3
  98.4 18.2 %collective-permute-done.17.refs_2_ = bf16[2272,256]{1,0:T(8,128)(2,1)} collective-permute-done((bf16[2272,256]{1,0:T(8,128)(2,1)}, bf16[2272,256]{1,0:T(8,128)(2,1)}, u32[]{:S(2)}, u32[]{:S(2)}) %collective-permute-start.17) | collective-permute-done | bytes 1163296 | tf_op jit(solution)/shard_map/ppermute | solution.py:511
  116.6 2.3 %collective-permute-done.22.refs_8_ = bf16[2272,256]{1,0:T(8,128)(2,1)} collective-permute-done((bf16[2272,256]{1,0:T(8,128)(2,1)}, bf16[2272,256]{1,0:T(8,128)(2,1)}, u32[]{:S(2)}, u32[]{:S(2)}) %collective-permute-start.22) | collective-permute-done | bytes 1163296 | tf_op jit(solution)/shard_map/ppermute | solution.py:511
  119.1 0.6 collective-permute-start.7
  119.9 0.7 convert_reduce_fusion.1.starts
  120.6 2.1 collective-permute-start.26
  122.7 0.6 pad_add_fusion.meta
  123.5 0.7 select_reduce_fusion.entries
  124.2 1.5 collective-permute-start.19
  125.8 2.2 %collective-permute-start.24 = (bf16[2272,256]{1,0:T(8,128)(2,1)}, bf16[2272,256]{1,0:T(8,128)(2,1)S(1)}, u32[]{:S(2)}, u32[]{:S(2)}) collective-permute-start(bf16[2272,256]{1,0:T(8,128)(2,1)} %collective-permute-done.21.refs_11_.refs_7_), channel_id=1, source_target_pairs={{0,96},{8,104},{16,112},{24,120},{32,0},{40,8},{48,16},{56,24},{64... | collective-permute-start | bytes 3489800 | tf_op jit(solution)/shard_map/ppermute | solution.py:511
  128.0 0.5 collective-permute-start.18
  128.5 0.6 copy-done.15
  129.1 1.1 copy-done.16
  130.2 21.9 %near.2 = (bf16[8,2048,256]{2,1,0:T(8,128)(2,1)}, f32[128,128]{1,0:T(8,128)}, f32[16,64,128]{2,1,0:T(8,128)}, f32[128,64,128]{2,1,0:T(8,128)}) custom-call(s32[2]{0:T(128)} %pad_add_fusion.meta, s32[16,16]{1,0:T(8,128)} %near.3, s32[4]{0:T(128)} %convert_reduce_fusion.1.starts, s32[384]{0:T(512)} %select_reduce_fusion.entries, ...), custom_call_target="tpu_custom_call" | custom-call | flops 8999999488 | bytes 30000000 | tf_op jit(solution)/shard_map/near/pallas_call | solution.py:359
  152.0 23.4 %shard_map.73.refs_11_ = f32[128,64,128]{2,1,0:T(8,128)} custom-call(s32[4]{0:T(128)} %convert_reduce_fusion.1.starts, s32[384]{0:T(512)} %select_reduce_fusion.entries, bf16[8,2048,256]{2,1,0:T(8,128)(2,1)} %get-tuple-element.18.x_hbm, f32[128,128]{1,0:T(8,128)} %get-tuple-element.19.norm_ref, ...), custom_call_target="tpu_custom_call" | custom-call | flops 10000000000 | bytes 25000000 | tf_op jit(solution)/shard_map/pallas_call | solution.py:467
  175.5 1.0 copy-done.3
  176.9 17.6 %shard_map.74 = (f32[64,64,128]{2,1,0:T(8,128)}, bf16[64,64,128]{2,1,0:T(8,128)(2,1)}) custom-call(s32[4]{0:T(128)} %convert_reduce_fusion.1.starts, s32[384]{0:T(512)} %select_reduce_fusion.entries, bf16[8,2048,256]{2,1,0:T(8,128)(2,1)} %get-tuple-element.18.x_hbm, f32[128,128]{1,0:T(8,128)} %get-tuple-element.19.norm_ref, bf16[2272,256]{1,0:T(8,128)(2,1)} %copy-done, ...), custom_call_target="tpu_custom_call" | custom-call | flops 5000000000 | bytes 25000000 | tf_op jit(solution)/shard_map/pallas_call | solution.py:467
  194.5 0.9 collective-permute-start.27
  195.4 2.5 %collective-permute-done.27 = bf16[64,64,128]{2,1,0:T(8,128)(2,1)S(1)} collective-permute-done((bf16[64,64,128]{2,1,0:T(8,128)(2,1)}, bf16[64,64,128]{2,1,0:T(8,128)(2,1)S(1)}, u32[]{:S(2)}, u32[]{:S(2)}) %collective-permute-start.27) | collective-permute-done | bytes 1048608 | tf_op jit(solution)/shard_map/ppermute | solution.py:511
  197.9 1.7 add_convert_fusion.2
  199.6 2.6 %collective-permute-start.28 = (bf16[16,64,128]{2,1,0:T(8,128)(2,1)S(1)}, bf16[16,64,128]{2,1,0:T(8,128)(2,1)S(1)}, u32[]{:S(2)}, u32[]{:S(2)}) collective-permute-start(bf16[16,64,128]{2,1,0:T(8,128)(2,1)S(1)} %get-tuple-element.25), channel_id=1, source_target_pairs={{0,4},{1,5},{2,6},{3,7},{4,0},{5,1},{6,2},{7,3},{8,12},{9,13},{10,... | collective-permute-start | bytes 786440 | tf_op jit(solution)/shard_map/ppermute | solution.py:511
  202.2 1.8 collective-permute-start.29
  204.0 0.7 collective-permute-start.30
  204.6 5.7 %collective-permute-done.28 = bf16[16,64,128]{2,1,0:T(8,128)(2,1)S(1)} collective-permute-done((bf16[16,64,128]{2,1,0:T(8,128)(2,1)S(1)}, bf16[16,64,128]{2,1,0:T(8,128)(2,1)S(1)}, u32[]{:S(2)}, u32[]{:S(2)}) %collective-permute-start.28) | collective-permute-done | bytes 262176 | tf_op jit(solution)/shard_map/ppermute | solution.py:511
  210.4 6.3 %collective-permute-done.29 = bf16[16,64,128]{2,1,0:T(8,128)(2,1)S(1)} collective-permute-done((bf16[16,64,128]{2,1,0:T(8,128)(2,1)S(1)}, bf16[16,64,128]{2,1,0:T(8,128)(2,1)S(1)}, u32[]{:S(2)}, u32[]{:S(2)}) %collective-permute-start.29) | collective-permute-done | bytes 262176 | tf_op jit(solution)/shard_map/ppermute | solution.py:511
  216.6 2.0 copy_bitcast_fusion
  (85 shorter events, 1.9 us)
Async XLA Ops:
  4.0 29.3 %collective-permute-start.10 = (bf16[1136,256]{1,0:T(8,128)(2,1)}, bf16[1136,256]{1,0:T(8,128)(2,1)S(1)}, u32[]{:S(2)}, u32[]{:S(2)}) collective-permute-start(bf16[1136,256]{1,0:T(8,128)(2,1)} %get-tuple-element.15), channel_id=1, source_target_pairs={{0,96},{8,104},{16,112},{24,120},{32,0},{40,8},{48,16},{56,24},{64... | collective-permute-start | bytes 1744904 | tf_op jit(solution)/shard_map/ppermute | solution.py:511
  8.2 26.8 %collective-permute-start.11 = (bf16[1136,256]{1,0:T(8,128)(2,1)}, bf16[1136,256]{1,0:T(8,128)(2,1)S(1)}, u32[]{:S(2)}, u32[]{:S(2)}) collective-permute-start(bf16[1136,256]{1,0:T(8,128)(2,1)} %get-tuple-element.15), channel_id=1, source_target_pairs={{0,64},{8,72},{16,80},{24,88},{32,96},{40,104},{48,112},{56,120},{... | collective-permute-start | bytes 1744904 | tf_op jit(solution)/shard_map/ppermute | solution.py:511
  8.2 26.8 %copy-start.13 = (bf16[2592,256]{1,0:T(8,128)(2,1)S(1)}, bf16[2592,256]{1,0:T(8,128)(2,1)}, u32[]{:S(2)}) copy-start(bf16[2592,256]{1,0:T(8,128)(2,1)} %get-tuple-element.14.refs_0_) | copy-start | bytes 3981316
  8.2 28.6 %collective-permute-start.13 = (bf16[1136,256]{1,0:T(8,128)(2,1)}, bf16[1136,256]{1,0:T(8,128)(2,1)S(1)}, u32[]{:S(2)}, u32[]{:S(2)}) collective-permute-start(bf16[1136,256]{1,0:T(8,128)(2,1)} %get-tuple-element.16), channel_id=1, source_target_pairs={{0,24},{8,0},{16,8},{24,16},{32,56},{40,32},{48,40},{56,48},{64,88... | collective-permute-start | bytes 1744904 | tf_op jit(solution)/shard_map/ppermute | solution.py:511
  11.0 25.9 %collective-permute-start.14 = (bf16[1136,256]{1,0:T(8,128)(2,1)}, bf16[1136,256]{1,0:T(8,128)(2,1)S(1)}, u32[]{:S(2)}, u32[]{:S(2)}) collective-permute-start(bf16[1136,256]{1,0:T(8,128)(2,1)} %get-tuple-element.16), channel_id=1, source_target_pairs={{0,16},{8,24},{16,0},{24,8},{32,48},{40,56},{48,32},{56,40},{64,80... | collective-permute-start | bytes 1744904 | tf_op jit(solution)/shard_map/ppermute | solution.py:511
  11.8 28.8 %collective-permute-start.9 = (bf16[1136,256]{1,0:T(8,128)(2,1)}, bf16[1136,256]{1,0:T(8,128)(2,1)S(1)}, u32[]{:S(2)}, u32[]{:S(2)}) collective-permute-start(bf16[1136,256]{1,0:T(8,128)(2,1)} %get-tuple-element.15), channel_id=1, source_target_pairs={{0,32},{8,40},{16,48},{24,56},{32,64},{40,72},{48,80},{56,88},{64,... | collective-permute-start | bytes 1744904 | tf_op jit(solution)/shard_map/ppermute | solution.py:511
  33.4 6.3 %copy-start.5 = (bf16[1136,256]{1,0:T(8,128)(2,1)S(1)}, bf16[1136,256]{1,0:T(8,128)(2,1)}, u32[]{:S(2)}) copy-start(bf16[1136,256]{1,0:T(8,128)(2,1)} %get-tuple-element.16) | copy-start | bytes 1744900
  33.4 31.4 %collective-permute-start = (bf16[2592,256]{1,0:T(8,128)(2,1)}, bf16[2592,256]{1,0:T(8,128)(2,1)S(1)}, u32[]{:S(2)}, u32[]{:S(2)}) collective-permute-start(bf16[2592,256]{1,0:T(8,128)(2,1)} %get-tuple-element.14.refs_0_), channel_id=1, source_target_pairs={{0,2},{1,3},{2,4},{3,5},{4,6},{5,7},{6,0},{7,1},{8,10},{9,11},{10,... | collective-permute-start | bytes 3981320 | tf_op jit(solution)/shard_map/ppermute | solution.py:511
  35.0 31.2 %collective-permute-start.1 = (bf16[2592,256]{1,0:T(8,128)(2,1)S(1)}, bf16[2592,256]{1,0:T(8,128)(2,1)S(1)}, u32[]{:S(2)}, u32[]{:S(2)}) collective-permute-start(bf16[2592,256]{1,0:T(8,128)(2,1)S(1)} %copy-done.13), channel_id=1, source_target_pairs={{0,6},{1,7},{2,0},{3,1},{4,2},{5,3},{6,4},{7,5},{8,14},{9,15},{10,... | collective-permute-start | bytes 3981320 | tf_op jit(solution)/shard_map/ppermute | solution.py:511
  36.8 29.6 %collective-permute-start.4 = (bf16[2592,256]{1,0:T(8,128)(2,1)S(1)}, bf16[2592,256]{1,0:T(8,128)(2,1)S(1)}, u32[]{:S(2)}, u32[]{:S(2)}) collective-permute-start(bf16[2592,256]{1,0:T(8,128)(2,1)S(1)} %copy-done.13), channel_id=1, source_target_pairs={{0,1},{1,0},{2,3},{3,2},{4,5},{5,4},{6,7},{7,6},{8,9},{9,8},{10,11... | collective-permute-start | bytes 3981320 | tf_op jit(solution)/shard_map/ppermute | solution.py:511
  36.8 27.9 %copy-start = (bf16[2272,256]{1,0:T(8,128)(2,1)}, bf16[2272,256]{1,0:T(8,128)(2,1)S(1)}, u32[]{:S(2)}) copy-start(bf16[2272,256]{1,0:T(8,128)(2,1)S(1)} %constant_dynamic-update-slice_fusion.2.refs_11_.refs_1_.refs_0_) | copy-start | bytes 3489796
  36.8 31.1 %collective-permute-start.16 = (bf16[2272,256]{1,0:T(8,128)(2,1)S(1)}, bf16[2272,256]{1,0:T(8,128)(2,1)S(1)}, u32[]{:S(2)}, u32[]{:S(2)}) collective-permute-start(bf16[2272,256]{1,0:T(8,128)(2,1)S(1)} %constant_dynamic-update-slice_fusion.2.refs_11_.refs_1_.refs_0_), channel_id=1, source_target_pairs={{0,24},{8,0},{16,8},{24,16},{32,56},{40,32},{48,40},{56,48},{64,88... | collective-permute-start | bytes 3489800 | tf_op jit(solution)/shard_map/ppermute | solution.py:511
  40.5 16.5 %collective-permute-start.12 = (bf16[1136,256]{1,0:T(8,128)(2,1)S(1)}, bf16[1136,256]{1,0:T(8,128)(2,1)S(1)}, u32[]{:S(2)}, u32[]{:S(2)}) collective-permute-start(bf16[1136,256]{1,0:T(8,128)(2,1)S(1)} %copy-done.5), channel_id=1, source_target_pairs={{0,8},{8,16},{16,24},{24,0},{32,40},{40,48},{48,56},{56,32},{64,72... | collective-permute-start | bytes 1744904 | tf_op jit(solution)/shard_map/ppermute | solution.py:511
  40.6 25.6 %copy-start.1 = (bf16[2272,256]{1,0:T(8,128)(2,1)}, bf16[2272,256]{1,0:T(8,128)(2,1)S(1)}, u32[]{:S(2)}) copy-start(bf16[2272,256]{1,0:T(8,128)(2,1)S(1)} %constant_dynamic-update-slice_fusion.6.refs_13_.refs_7_.refs_5_) | copy-start | bytes 3489796
  57.0 28.0 %collective-permute-start.21 = (bf16[2272,256]{1,0:T(8,128)(2,1)S(1)}, bf16[2272,256]{1,0:T(8,128)(2,1)}, u32[]{:S(2)}, u32[]{:S(2)}) collective-permute-start(bf16[2272,256]{1,0:T(8,128)(2,1)S(1)} %constant_dynamic-update-slice_fusion.6.refs_13_.refs_7_.refs_5_), channel_id=1, source_target_pairs={{0,96},{8,104},{16,112},{24,120},{32,0},{40,8},{48,16},{56,24},{64... | collective-permute-start | bytes 3489800 | tf_op jit(solution)/shard_map/ppermute | solution.py:511
  64.8 20.3 %copy-start.7 = (bf16[2592,256]{1,0:T(8,128)(2,1)}, bf16[2592,256]{1,0:T(8,128)(2,1)S(1)}, u32[]{:S(2)}) copy-start(bf16[2592,256]{1,0:T(8,128)(2,1)S(1)} %collective-permute-done.refs_1_) | copy-start | bytes 3981316
  64.8 29.8 %collective-permute-start.15 = (bf16[2272,256]{1,0:T(8,128)(2,1)S(1)}, bf16[2272,256]{1,0:T(8,128)(2,1)}, u32[]{:S(2)}, u32[]{:S(2)}) collective-permute-start(bf16[2272,256]{1,0:T(8,128)(2,1)S(1)} %constant_dynamic-update-slice_fusion.2.refs_11_.refs_1_.refs_0_), channel_id=1, source_target_pairs={{0,8},{8,16},{16,24},{24,0},{32,40},{40,48},{48,56},{56,32},{64,72... | collective-permute-start | bytes 3489800 | tf_op jit(solution)/shard_map/ppermute | solution.py:511
  66.2 18.8 %copy-start.9 = (bf16[2592,256]{1,0:T(8,128)(2,1)}, bf16[2592,256]{1,0:T(8,128)(2,1)S(1)}, u32[]{:S(2)}) copy-start(bf16[2592,256]{1,0:T(8,128)(2,1)S(1)} %collective-permute-done.1.refs_2_) | copy-start | bytes 3981316
  66.3 30.4 %collective-permute-start.20 = (bf16[2272,256]{1,0:T(8,128)(2,1)S(1)}, bf16[2272,256]{1,0:T(8,128)(2,1)}, u32[]{:S(2)}, u32[]{:S(2)}) collective-permute-start(bf16[2272,256]{1,0:T(8,128)(2,1)S(1)} %constant_dynamic-update-slice_fusion.6.refs_13_.refs_7_.refs_5_), channel_id=1, source_target_pairs={{0,32},{8,40},{16,48},{24,56},{32,64},{40,72},{48,80},{56,88},{64,... | collective-permute-start | bytes 3489800 | tf_op jit(solution)/shard_map/ppermute | solution.py:511
  66.3 18.7 %copy-start.14 = (bf16[2592,256]{1,0:T(8,128)(2,1)}, bf16[2592,256]{1,0:T(8,128)(2,1)S(1)}, u32[]{:S(2)}) copy-start(bf16[2592,256]{1,0:T(8,128)(2,1)S(1)} %collective-permute-done.4.refs_5_) | copy-start | bytes 3981316
  66.4 50.2 %collective-permute-start.17 = (bf16[2272,256]{1,0:T(8,128)(2,1)}, bf16[2272,256]{1,0:T(8,128)(2,1)}, u32[]{:S(2)}, u32[]{:S(2)}) collective-permute-start(bf16[2272,256]{1,0:T(8,128)(2,1)} %constant_dynamic-update-slice_fusion.refs_10_.refs_0_), channel_id=1, source_target_pairs={{0,8},{8,16},{16,24},{24,0},{32,40},{40,48},{48,56},{56,32},{64,72... | collective-permute-start | bytes 3489800 | tf_op jit(solution)/shard_map/ppermute | solution.py:511
  67.9 56.3 %copy-start.2 = (bf16[2272,256]{1,0:T(8,128)(2,1)}, bf16[2272,256]{1,0:T(8,128)(2,1)S(1)}, u32[]{:S(2)}) copy-start(bf16[2272,256]{1,0:T(8,128)(2,1)S(1)} %collective-permute-done.16.refs_5_.refs_2_) | copy-start | bytes 3489796
  67.9 51.0 %collective-permute-start.22 = (bf16[2272,256]{1,0:T(8,128)(2,1)}, bf16[2272,256]{1,0:T(8,128)(2,1)}, u32[]{:S(2)}, u32[]{:S(2)}) collective-permute-start(bf16[2272,256]{1,0:T(8,128)(2,1)} %constant_dynamic-update-slice_fusion.4.refs_12_.refs_6_), channel_id=1, source_target_pairs={{0,32},{8,40},{16,48},{24,56},{32,64},{40,72},{48,80},{56,88},{64,... | collective-permute-start | bytes 3489800 | tf_op jit(solution)/shard_map/ppermute | solution.py:511
  85.0 35.6 %collective-permute-start.25 = (bf16[2272,256]{1,0:T(8,128)(2,1)}, bf16[2272,256]{1,0:T(8,128)(2,1)}, u32[]{:S(2)}, u32[]{:S(2)}) collective-permute-start(bf16[2272,256]{1,0:T(8,128)(2,1)} %constant_dynamic-update-slice_fusion.refs_10_.refs_0_), channel_id=1, source_target_pairs={{0,24},{8,0},{16,8},{24,16},{32,56},{40,32},{48,40},{56,48},{64,88... | collective-permute-start | bytes 3489800 | tf_op jit(solution)/shard_map/ppermute | solution.py:511
  85.1 1.5 copy-start.10
  85.1 31.5 %copy-start.8 = (bf16[2592,256]{1,0:T(8,128)(2,1)S(1)}, bf16[2592,256]{1,0:T(8,128)(2,1)}, u32[]{:S(2)}) copy-start(bf16[2592,256]{1,0:T(8,128)(2,1)} %copy-done.7) | copy-start | bytes 3981316
  85.1 33.8 %copy-start.11 = (s32[128,3,1]{0,2,1:T(1,128)S(1)}, s32[128,3,1]{0,2,1:T(1,128)}, u32[]{:S(2)}) copy-start(s32[128,3,1]{0,2,1:T(1,128)} %param.10) | copy-start | bytes 4612
  85.1 33.9 %copy-start.12 = (s32[112]{0:T(128)S(1)}, s32[112]{0:T(128)}, u32[]{:S(2)}) copy-start(s32[112]{0:T(128)} %constant.94.clone) | copy-start | bytes 1348
  94.6 24.5 %collective-permute-start.2 = (bf16[1296,256]{1,0:T(8,128)(2,1)S(1)}, bf16[1296,256]{1,0:T(8,128)(2,1)S(1)}, u32[]{:S(2)}, u32[]{:S(2)}) collective-permute-start(bf16[1296,256]{1,0:T(8,128)(2,1)S(1)} %slice.48), channel_id=1, source_target_pairs={{0,2},{1,3},{2,4},{3,5},{4,6},{5,7},{6,0},{7,1},{8,10},{9,11},{10,... | collective-permute-start | bytes 1990664 | tf_op jit(solution)/shard_map/ppermute | solution.py:511
  96.6 23.1 %collective-permute-start.3 = (bf16[1296,256]{1,0:T(8,128)(2,1)S(1)}, bf16[1296,256]{1,0:T(8,128)(2,1)S(1)}, u32[]{:S(2)}, u32[]{:S(2)}) collective-permute-start(bf16[1296,256]{1,0:T(8,128)(2,1)S(1)} %slice.49), channel_id=1, source_target_pairs={{0,6},{1,7},{2,0},{3,1},{4,2},{5,3},{6,4},{7,5},{8,14},{9,15},{10,... | collective-permute-start | bytes 1990664 | tf_op jit(solution)/shard_map/ppermute | solution.py:511
  116.6 11.4 %collective-permute-start.5 = (bf16[2592,256]{1,0:T(8,128)(2,1)S(1)}, bf16[2592,256]{1,0:T(8,128)(2,1)S(1)}, u32[]{:S(2)}, u32[]{:S(2)}) collective-permute-start(bf16[2592,256]{1,0:T(8,128)(2,1)S(1)} %copy-done.8), channel_id=1, source_target_pairs={{0,1},{1,0},{2,3},{3,2},{4,5},{5,4},{6,7},{7,6},{8,9},{9,8},{10,11... | collective-permute-start | bytes 3981320 | tf_op jit(solution)/shard_map/ppermute | solution.py:511
  118.9 9.6 %collective-permute-start.6 = (bf16[2592,256]{1,0:T(8,128)(2,1)S(1)}, bf16[2592,256]{1,0:T(8,128)(2,1)S(1)}, u32[]{:S(2)}, u32[]{:S(2)}) collective-permute-start(bf16[2592,256]{1,0:T(8,128)(2,1)S(1)} %copy-done.10), channel_id=1, source_target_pairs={{0,1},{1,0},{2,3},{3,2},{4,5},{5,4},{6,7},{7,6},{8,9},{9,8},{10,11... | collective-permute-start | bytes 3981320 | tf_op jit(solution)/shard_map/ppermute | solution.py:511
  119.1 9.4 %copy-start.17 = (bf16[1296,256]{1,0:T(8,128)(2,1)}, bf16[1296,256]{1,0:T(8,128)(2,1)S(1)}, u32[]{:S(2)}) copy-start(bf16[1296,256]{1,0:T(8,128)(2,1)S(1)} %collective-permute-done.2.refs_3_) | copy-start | bytes 1990660
  119.1 5.1 %collective-permute-start.7 = (bf16[1296,256]{1,0:T(8,128)(2,1)S(1)}, bf16[1296,256]{1,0:T(8,128)(2,1)S(1)}, u32[]{:S(2)}, u32[]{:S(2)}) collective-permute-start(bf16[1296,256]{1,0:T(8,128)(2,1)S(1)} %collective-permute-done.2.refs_3_), channel_id=1, source_target_pairs={{0,1},{1,0},{2,3},{3,2},{4,5},{5,4},{6,7},{7,6},{8,9},{9,8},{10,11... | collective-permute-start | bytes 1990664 | tf_op jit(solution)/shard_map/ppermute | solution.py:511
  119.7 8.8 %copy-start.18 = (bf16[1296,256]{1,0:T(8,128)(2,1)}, bf16[1296,256]{1,0:T(8,128)(2,1)S(1)}, u32[]{:S(2)}) copy-start(bf16[1296,256]{1,0:T(8,128)(2,1)S(1)} %collective-permute-done.3.refs_4_) | copy-start | bytes 1990660
  119.7 6.1 %collective-permute-start.8 = (bf16[1296,256]{1,0:T(8,128)(2,1)S(1)}, bf16[1296,256]{1,0:T(8,128)(2,1)S(1)}, u32[]{:S(2)}, u32[]{:S(2)}) collective-permute-start(bf16[1296,256]{1,0:T(8,128)(2,1)S(1)} %collective-permute-done.3.refs_4_), channel_id=1, source_target_pairs={{0,1},{1,0},{2,3},{3,2},{4,5},{5,4},{6,7},{7,6},{8,9},{9,8},{10,11... | collective-permute-start | bytes 1990664 | tf_op jit(solution)/shard_map/ppermute | solution.py:511
  120.6 31.4 %collective-permute-start.26 = (bf16[2272,256]{1,0:T(8,128)(2,1)}, bf16[2272,256]{1,0:T(8,128)(2,1)}, u32[]{:S(2)}, u32[]{:S(2)}) collective-permute-start(bf16[2272,256]{1,0:T(8,128)(2,1)} %constant_dynamic-update-slice_fusion.4.refs_12_.refs_6_), channel_id=1, source_target_pairs={{0,96},{8,104},{16,112},{24,120},{32,0},{40,8},{48,16},{56,24},{64... | collective-permute-start | bytes 3489800 | tf_op jit(solution)/shard_map/ppermute | solution.py:511
  124.2 4.3 %copy-start.19 = (bf16[1296,256]{1,0:T(8,128)(2,1)}, bf16[1296,256]{1,0:T(8,128)(2,1)S(1)}, u32[]{:S(2)}) copy-start(bf16[1296,256]{1,0:T(8,128)(2,1)S(1)} %collective-permute-done.7.refs_8_) | copy-start | bytes 1990660
  124.2 51.2 %collective-permute-start.19 = (bf16[2272,256]{1,0:T(8,128)(2,1)S(1)}, bf16[2272,256]{1,0:T(8,128)(2,1)S(1)}, u32[]{:S(2)}, u32[]{:S(2)}) collective-permute-start(bf16[2272,256]{1,0:T(8,128)(2,1)S(1)} %collective-permute-done.16.refs_5_.refs_2_), channel_id=1, source_target_pairs={{0,24},{8,0},{16,8},{24,16},{32,56},{40,32},{48,40},{56,48},{64,88... | collective-permute-start | bytes 3489800 | tf_op jit(solution)/shard_map/ppermute | solution.py:511
  125.8 2.7 %copy-start.20 = (bf16[1296,256]{1,0:T(8,128)(2,1)}, bf16[1296,256]{1,0:T(8,128)(2,1)S(1)}, u32[]{:S(2)}) copy-start(bf16[1296,256]{1,0:T(8,128)(2,1)S(1)} %collective-permute-done.8.refs_9_) | copy-start | bytes 1990660
  125.8 49.7 %collective-permute-start.24 = (bf16[2272,256]{1,0:T(8,128)(2,1)}, bf16[2272,256]{1,0:T(8,128)(2,1)S(1)}, u32[]{:S(2)}, u32[]{:S(2)}) collective-permute-start(bf16[2272,256]{1,0:T(8,128)(2,1)} %collective-permute-done.21.refs_11_.refs_7_), channel_id=1, source_target_pairs={{0,96},{8,104},{16,112},{24,120},{32,0},{40,8},{48,16},{56,24},{64... | collective-permute-start | bytes 3489800 | tf_op jit(solution)/shard_map/ppermute | solution.py:511
  128.0 47.5 %collective-permute-start.18 = (bf16[2272,256]{1,0:T(8,128)(2,1)}, bf16[2272,256]{1,0:T(8,128)(2,1)}, u32[]{:S(2)}, u32[]{:S(2)}) collective-permute-start(bf16[2272,256]{1,0:T(8,128)(2,1)} %collective-permute-done.17.refs_2_), channel_id=1, source_target_pairs={{0,8},{8,16},{16,24},{24,0},{32,40},{40,48},{48,56},{56,32},{64,72... | collective-permute-start | bytes 3489800 | tf_op jit(solution)/shard_map/ppermute | solution.py:511
  130.1 45.4 %collective-permute-start.23 = (bf16[2272,256]{1,0:T(8,128)(2,1)}, bf16[2272,256]{1,0:T(8,128)(2,1)}, u32[]{:S(2)}, u32[]{:S(2)}) collective-permute-start(bf16[2272,256]{1,0:T(8,128)(2,1)} %collective-permute-done.22.refs_8_), channel_id=1, source_target_pairs={{0,32},{8,40},{16,48},{24,56},{32,64},{40,72},{48,80},{56,88},{64,... | collective-permute-start | bytes 3489800 | tf_op jit(solution)/shard_map/ppermute | solution.py:511
  194.5 3.4 %collective-permute-start.27 = (bf16[64,64,128]{2,1,0:T(8,128)(2,1)}, bf16[64,64,128]{2,1,0:T(8,128)(2,1)S(1)}, u32[]{:S(2)}, u32[]{:S(2)}) collective-permute-start(bf16[64,64,128]{2,1,0:T(8,128)(2,1)} %get-tuple-element.22), channel_id=1, source_target_pairs={{0,1},{1,0},{2,3},{3,2},{4,5},{5,4},{6,7},{7,6},{8,9},{9,8},{10,11... | collective-permute-start | bytes 3145736 | tf_op jit(solution)/shard_map/ppermute | solution.py:511
  197.9 18.7 %copy-start.6 = (f32[16,64,128]{2,1,0:T(8,128)S(1)}, f32[16,64,128]{2,1,0:T(8,128)}, u32[]{:S(2)}) copy-start(f32[16,64,128]{2,1,0:T(8,128)} %get-tuple-element.17) | copy-start | bytes 1572868
  199.6 10.8 %collective-permute-start.28 = (bf16[16,64,128]{2,1,0:T(8,128)(2,1)S(1)}, bf16[16,64,128]{2,1,0:T(8,128)(2,1)S(1)}, u32[]{:S(2)}, u32[]{:S(2)}) collective-permute-start(bf16[16,64,128]{2,1,0:T(8,128)(2,1)S(1)} %get-tuple-element.25), channel_id=1, source_target_pairs={{0,4},{1,5},{2,6},{3,7},{4,0},{5,1},{6,2},{7,3},{8,12},{9,13},{10,... | collective-permute-start | bytes 786440 | tf_op jit(solution)/shard_map/ppermute | solution.py:511
  202.2 14.4 %collective-permute-start.29 = (bf16[16,64,128]{2,1,0:T(8,128)(2,1)S(1)}, bf16[16,64,128]{2,1,0:T(8,128)(2,1)S(1)}, u32[]{:S(2)}, u32[]{:S(2)}) collective-permute-start(bf16[16,64,128]{2,1,0:T(8,128)(2,1)S(1)} %get-tuple-element.27), channel_id=1, source_target_pairs={{0,6},{1,7},{2,0},{3,1},{4,2},{5,3},{6,4},{7,5},{8,14},{9,15},{10,... | collective-permute-start | bytes 786440 | tf_op jit(solution)/shard_map/ppermute | solution.py:511
  204.0 12.6 %collective-permute-start.30 = (bf16[16,64,128]{2,1,0:T(8,128)(2,1)S(1)}, bf16[16,64,128]{2,1,0:T(8,128)(2,1)S(1)}, u32[]{:S(2)}, u32[]{:S(2)}) collective-permute-start(bf16[16,64,128]{2,1,0:T(8,128)(2,1)S(1)} %get-tuple-element.26), channel_id=1, source_target_pairs={{0,2},{1,3},{2,4},{3,5},{4,6},{5,7},{6,0},{7,1},{8,10},{9,11},{10,... | collective-permute-start | bytes 786440 | tf_op jit(solution)/shard_map/ppermute | solution.py:511
  (4 other events, 4.6 us)
where the time goes:
time: 219 us
  waiting for transfers between devices  99 us (45%)
  Pallas kernels  66.9 us (31%)
  starting transfers between devices  36.9 us (17%)
  local copies, waits for them, and re-layouts  9.32 us (4%)
  other arithmetic  6.22 us (3%)
    ppermute x31, waiting for transfers between devices, move(): return lax.ppermute(v, axis, pairs)  99 us
    pallas_call x2, Pallas kernels, far_call(): pl.pallas_call(body, grid_spec=pltpu.PrefetchScalarGridSpec(num_scalar_pr...  41 us
    ppermute x31, starting transfers between devices, move(): return lax.ppermute(v, axis, pairs)  36.9 us
    pallas_call x1, Pallas kernels, near_call(): pl.pallas_call(body, grid_spec=pltpu.PrefetchScalarGridSpec(num_scalar_pr...  21.9 us
    unnamed x46, local copies, waits for them, and re-layouts  6.1 us
  transfers between devices with their start and end apart: 31, of which 11 were waited for; matrix products, arithmetic and copies ran while one was open for 4% of the time, Pallas kernels for 21%

commit v1 on v0

--- a/solution.py
+++ b/solution.py
@@ -354,7 +354,7 @@
             store(k).wait()
         result.wait()
 
-    anys = pl.BlockSpec(memory_space=pl.ANY)
+    anys = pl.BlockSpec(memory_space=pltpu.HBM)
     vm = pl.BlockSpec(memory_space=pltpu.VMEM)
     return pl.pallas_call(
         body,
@@ -393,27 +393,27 @@
     )(meta, near_list, starts, entries, *pieces, *panels)
 
 
-def far_call(group, starts, entries, x_all, norms, accs, panels, rows, nrows):
-    count, extra = len(panels), len(accs)
-    last = extra > 0
+def far_call(group, starts, entries, x_all, norms, acc, panels, rows, nrows):
+    count = len(panels)
+    last = group == 2
 
     def body(starts, entries, x_hbm, norm_ref, *refs):
-        sources, sums, refs = refs[:count], refs[count : count + extra], refs[count + extra :]
+        sources, acc_hbm, refs = refs[:count], refs[count], refs[count + 1 :]
         if last:
-            keep_hbm, send_hbm, *refs, acc_v, send_v = refs
+            keep_hbm, send_hbm, *refs, send_v = refs
         else:
             out_hbm, *refs = refs
-        out_v, xs, pan, parts, wide, node_norms, s0, s1, psem, xsem, osem = refs
+        out_v, acc_v, xs, pan, parts, wide, node_norms, s0, s1, psem, xsem, osem = refs
         panel_copies = [
             pltpu.make_async_copy(sources[p].at[pl.ds(a, r), :], to.at[pl.ds(d, r), :], psem.at[i])
             for i, (to, p, a, r, d) in enumerate([(pan, *item) for item in rows] + [(parts, *item) for item in nrows])
         ]
-        acc_copies = [pltpu.make_async_copy(sums[i], acc_v.at[i], osem.at[i]) for i in range(extra)]
+        acc_copy = pltpu.make_async_copy(acc_hbm, acc_v, osem.at[0])
 
         def x_copy(k):
             return pltpu.make_async_copy(x_hbm.at[k], xs.at[pl.ds(k * PTS, PTS), :], xsem.at[k])
 
-        for copy in panel_copies + [x_copy(k) for k in range(8)] + acc_copies:
+        for copy in panel_copies + [x_copy(k) for k in range(8)] + [acc_copy]:
             copy.start()
 
         def clear(b, carry):
@@ -434,17 +434,20 @@
             return jnp.maximum(done, upto)
 
         run_far(group, starts, entries, xs, norm_ref, pan, node_norms, out_v, s0, s1, arrive)
+        acc_copy.wait()
+
+        def merge_first(blocks, first=0):
+            def merge_one(b, carry):
+                out_v[first + b] = out_v[first + b] + acc_v[first + b]
+                return carry
+
+            lax.fori_loop(0, blocks, merge_one, 0)
+
         if last:
-            for copy in acc_copies:
-                copy.wait()
 
             def merge(b, carry):
                 c = BLOCKS // 2 + b
-                send_v[b] = (out_v[c] + (acc_v[0, c] + acc_v[1, c])).astype(BF16)
-                return carry
-
-            def merge_kept(b, carry):
-                out_v[b] = out_v[b] + (acc_v[0, b] + acc_v[1, b])
+                send_v[b] = (out_v[c] + acc_v[c]).astype(BF16)
                 return carry
 
             copies = [
@@ -453,15 +456,19 @@
             ]
             lax.fori_loop(0, BLOCKS // 2, merge, 0)
             copies[0].start()
-            lax.fori_loop(0, BLOCKS // 2, merge_kept, 0)
+            merge_first(BLOCKS // 2)
             copies[1].start()
         else:
-            copies = [pltpu.make_async_copy(out_v.at[pl.ds(0, BLOCKS)], out_hbm, osem.at[0])]
-            copies[0].start()
+            copies = []
+            for part in range(4):
+                merge_first(BLOCKS // 4, part * BLOCKS // 4)
+                rows_out = pl.ds(part * BLOCKS // 4, BLOCKS // 4)
+                copies.append(pltpu.make_async_copy(out_v.at[rows_out], out_hbm.at[rows_out], osem.at[part]))
+                copies[-1].start()
         for copy in copies:
             copy.wait()
 
-    anys = pl.BlockSpec(memory_space=pl.ANY)
+    anys = pl.BlockSpec(memory_space=pltpu.HBM)
     sums = (BLOCKS, WCOL, BLK)
     half = (BLOCKS // 2, WCOL, BLK)
     return pl.pallas_call(
@@ -469,10 +476,11 @@
         grid_spec=pltpu.PrefetchScalarGridSpec(
             num_scalar_prefetch=2,
             grid=(),
-            in_specs=[anys, pl.BlockSpec(memory_space=pltpu.VMEM)] + [anys] * (count + extra),
+            in_specs=[anys, pl.BlockSpec(memory_space=pltpu.VMEM)] + [anys] * (count + 1),
             out_specs=(anys, anys) if last else anys,
             scratch_shapes=[
                 pltpu.VMEM((BLOCKS + 1, WCOL, BLK), F32),
+                pltpu.VMEM(sums, F32),
                 pltpu.VMEM((8 * PTS, E), BF16),
                 pltpu.VMEM((panel_nodes(group) * NODE, E), BF16),
                 pltpu.VMEM((len(nrows) * 16, E), BF16),
@@ -482,9 +490,9 @@
                 pltpu.VMEM((GROUP, BLK, RANK), F32),
                 pltpu.SemaphoreType.DMA((len(rows) + len(nrows),)),
                 pltpu.SemaphoreType.DMA((8,)),
-                pltpu.SemaphoreType.DMA((2,)),
+                pltpu.SemaphoreType.DMA((4,)),
             ]
-            + ([pltpu.VMEM((extra, *sums), F32), pltpu.VMEM(half, BF16)] if last else []),
+            + ([pltpu.VMEM(half, BF16)] if last else []),
         ),
         out_shape=(jax.ShapeDtypeStruct(half, F32), jax.ShapeDtypeStruct(half, BF16))
         if last
@@ -492,7 +500,7 @@
         cost_estimate=pl.CostEstimate(
             flops=(5 if last else 10) * 10**9, bytes_accessed=25 * 10**6, transcendentals=6 * 10**6
         ),
-    )(starts, entries, x_all, norms, *panels, *accs)
+    )(starts, entries, x_all, norms, *panels, acc)
 
 
 def shards(points, weights, near_list, far_list, skel_index, equiv_weights):
@@ -538,15 +546,14 @@
         return [panels[u] for u in used], *copies
 
     x_all, norms, near_sum, sums0 = near_call(meta, near_list, starts, entries, pieces, *operands(0))
-    sums1 = far_call(1, starts, entries, x_all, norms, [], *operands(1))
-    keep, send = far_call(2, starts, entries, x_all, norms, [sums0, sums1], *operands(2))
+    sums1 = far_call(1, starts, entries, x_all, norms, sums0, *operands(1))
+    keep, send = far_call(2, starts, entries, x_all, norms, sums1, *operands(2))
 
     half = (4, BLK_DEV, WCOL, BLK)
-    keep, got = keep.reshape(half), move(send, "src", partner).reshape(half)
-    out = near_sum + keep[0] + got[0].astype(F32)
-    for i, d in ((3, 2), (1, -1), (2, 1)):
-        chip = (keep[i] + got[i].astype(F32)).astype(BF16)
-        out = out + move(chip, "src", along_y(d)).astype(F32)
+    chip = keep.reshape(half) + move(send, "src", partner).reshape(half).astype(F32)
+    out = near_sum + chip[0]
+    for i, d in ((1, -1), (2, 1), (3, 2)):
+        out = out + move(chip[i].astype(BF16), "src", along_y(d)).astype(F32)
     return out.transpose(0, 2, 1).reshape(PTS, WCOL)
 
 

time: 219 us -> 220 us (level)
  no operation moved by 1% of the time
where the time goes in v1:
time: 220 us
  waiting for transfers between devices  100 us (45%)
  Pallas kernels  66.8 us (30%)
  starting transfers between devices  37.6 us (17%)
  local copies, waits for them, and re-layouts  9.41 us (4%)
  other arithmetic  5.42 us (2%)
    ppermute x31, waiting for transfers between devices, move(): return lax.ppermute(v, axis, pairs)  100 us
    pallas_call x2, Pallas kernels, far_call(): pl.pallas_call(body, grid_spec=pltpu.PrefetchScalarGridSpec(num_scalar_pr...  40.9 us
    ppermute x31, starting transfers between devices, move(): return lax.ppermute(v, axis, pairs)  37.6 us
    pallas_call x1, Pallas kernels, near_call(): pl.pallas_call(body, grid_spec=pltpu.PrefetchScalarGridSpec(num_scalar_pr...  21.8 us
    unnamed x46, local copies, waits for them, and re-layouts  6.18 us
  transfers between devices with their start and end apart: 31, of which 11 were waited for; matrix products, arithmetic and copies ran while one was open for 4% of the time, Pallas kernels for 21%

profile of v1, /device:TPU:0, one launch (start us, length us, event | category | flops | bytes accessed | tf_op | source)
XLA Modules:
  0.0 219.9 jit_solution(8821551677823417119)
XLA Ops:
  0.0 4.1 %prep.1 = (bf16[2592,256]{1,0:T(8,128)(2,1)}, bf16[1136,256]{1,0:T(8,128)(2,1)}, bf16[1136,256]{1,0:T(8,128)(2,1)}) custom-call(bf16[2048,256]{1,0:T(8,128)(2,1)} %pts.1, bf16[64,2048]{1,0:T(8,128)(2,1)} %bitcast.88, bf16[7,64,256]{2,1,0:T(8,128)(2,1)} %bitcast.89, s32[7,256]{1,0:T(8,128)} %idx.1), custom_call_target="tpu_custom_call" | custom-call | flops 1000000000 | bytes 8000000 | tf_op jit(solution)/shard_map/prep/pallas_call | solution.py:105
  4.1 4.1 %collective-permute-start.10 = (bf16[1136,256]{1,0:T(8,128)(2,1)}, bf16[1136,256]{1,0:T(8,128)(2,1)S(1)}, u32[]{:S(2)}, u32[]{:S(2)}) collective-permute-start(bf16[1136,256]{1,0:T(8,128)(2,1)} %get-tuple-element.15), channel_id=1, source_target_pairs={{0,96},{8,104},{16,112},{24,120},{32,0},{40,8},{48,16},{56,24},{64... | collective-permute-start | bytes 1744904 | tf_op jit(solution)/shard_map/ppermute | solution.py:519
  8.3 2.8 %collective-permute-start.13 = (bf16[1136,256]{1,0:T(8,128)(2,1)}, bf16[1136,256]{1,0:T(8,128)(2,1)S(1)}, u32[]{:S(2)}, u32[]{:S(2)}) collective-permute-start(bf16[1136,256]{1,0:T(8,128)(2,1)} %get-tuple-element.16), channel_id=1, source_target_pairs={{0,24},{8,0},{16,8},{24,16},{32,56},{40,32},{48,40},{56,48},{64,88... | collective-permute-start | bytes 1744904 | tf_op jit(solution)/shard_map/ppermute | solution.py:519
  11.0 0.8 collective-permute-start.14
  11.8 1.3 collective-permute-start.9
  13.1 2.0 constant_dynamic-update-slice_fusion.1
  15.1 18.4 %collective-permute-done.10 = bf16[1136,256]{1,0:T(8,128)(2,1)S(1)} collective-permute-done((bf16[1136,256]{1,0:T(8,128)(2,1)}, bf16[1136,256]{1,0:T(8,128)(2,1)S(1)}, u32[]{:S(2)}, u32[]{:S(2)}) %collective-permute-start.10) | collective-permute-done | bytes 581664 | tf_op jit(solution)/shard_map/ppermute | solution.py:519
  33.5 1.6 collective-permute-start
  35.1 1.7 collective-permute-start.1
  36.9 2.8 %collective-permute-start.16 = (bf16[2272,256]{1,0:T(8,128)(2,1)S(1)}, bf16[2272,256]{1,0:T(8,128)(2,1)S(1)}, u32[]{:S(2)}, u32[]{:S(2)}) collective-permute-start(bf16[2272,256]{1,0:T(8,128)(2,1)S(1)} %constant_dynamic-update-slice_fusion.2.refs_11_.refs_1_.refs_0_), channel_id=1, source_target_pairs={{0,24},{8,0},{16,8},{24,16},{32,56},{40,32},{48,40},{56,48},{64,88... | collective-permute-start | bytes 3489800 | tf_op jit(solution)/shard_map/ppermute | solution.py:519
  39.7 0.9 constant_dynamic-update-slice_fusion.5
  40.8 0.9 constant_dynamic-update-slice_fusion.refs_10_.refs_0_
  41.7 15.5 %collective-permute-done.12 = bf16[1136,256]{1,0:T(8,128)(2,1)S(1)} collective-permute-done((bf16[1136,256]{1,0:T(8,128)(2,1)S(1)}, bf16[1136,256]{1,0:T(8,128)(2,1)S(1)}, u32[]{:S(2)}, u32[]{:S(2)}) %collective-permute-start.12) | collective-permute-done | bytes 581664 | tf_op jit(solution)/shard_map/ppermute | solution.py:519
  57.1 3.6 %collective-permute-start.21 = (bf16[2272,256]{1,0:T(8,128)(2,1)S(1)}, bf16[2272,256]{1,0:T(8,128)(2,1)}, u32[]{:S(2)}, u32[]{:S(2)}) collective-permute-start(bf16[2272,256]{1,0:T(8,128)(2,1)S(1)} %constant_dynamic-update-slice_fusion.6.refs_13_.refs_7_.refs_5_), channel_id=1, source_target_pairs={{0,96},{8,104},{16,112},{24,120},{32,0},{40,8},{48,16},{56,24},{64... | collective-permute-start | bytes 3489800 | tf_op jit(solution)/shard_map/ppermute | solution.py:519
  60.7 0.9 constant_dynamic-update-slice_fusion.4.refs_12_.refs_6_
  61.6 3.2 %collective-permute-done.refs_1_ = bf16[2592,256]{1,0:T(8,128)(2,1)S(1)} collective-permute-done((bf16[2592,256]{1,0:T(8,128)(2,1)}, bf16[2592,256]{1,0:T(8,128)(2,1)S(1)}, u32[]{:S(2)}, u32[]{:S(2)}) %collective-permute-start) | collective-permute-done | bytes 1327136 | tf_op jit(solution)/shard_map/ppermute | solution.py:519
  64.8 1.5 collective-permute-start.15
  66.4 1.6 collective-permute-start.17
  68.0 17.1 %collective-permute-done.21.refs_11_.refs_7_ = bf16[2272,256]{1,0:T(8,128)(2,1)} collective-permute-done((bf16[2272,256]{1,0:T(8,128)(2,1)S(1)}, bf16[2272,256]{1,0:T(8,128)(2,1)}, u32[]{:S(2)}, u32[]{:S(2)}) %collective-permute-start.21) | collective-permute-done | bytes 1163296 | tf_op jit(solution)/shard_map/ppermute | solution.py:519
  85.3 1.3 slice.31
  86.8 7.9 %collective-permute-done.15.refs_3_.refs_1_ = bf16[2272,256]{1,0:T(8,128)(2,1)} collective-permute-done((bf16[2272,256]{1,0:T(8,128)(2,1)S(1)}, bf16[2272,256]{1,0:T(8,128)(2,1)}, u32[]{:S(2)}, u32[]{:S(2)}) %collective-permute-start.15) | collective-permute-done | bytes 1163296 | tf_op jit(solution)/shard_map/ppermute | solution.py:519
  94.9 1.8 collective-permute-done.20.refs_9_.refs_6_
  96.7 1.7 collective-permute-start.3
  98.4 18.2 %collective-permute-done.17.refs_2_ = bf16[2272,256]{1,0:T(8,128)(2,1)} collective-permute-done((bf16[2272,256]{1,0:T(8,128)(2,1)}, bf16[2272,256]{1,0:T(8,128)(2,1)}, u32[]{:S(2)}, u32[]{:S(2)}) %collective-permute-start.17) | collective-permute-done | bytes 1163296 | tf_op jit(solution)/shard_map/ppermute | solution.py:519
  116.6 2.3 %collective-permute-done.22.refs_8_ = bf16[2272,256]{1,0:T(8,128)(2,1)} collective-permute-done((bf16[2272,256]{1,0:T(8,128)(2,1)}, bf16[2272,256]{1,0:T(8,128)(2,1)}, u32[]{:S(2)}, u32[]{:S(2)}) %collective-permute-start.22) | collective-permute-done | bytes 1163296 | tf_op jit(solution)/shard_map/ppermute | solution.py:519
  119.2 0.6 collective-permute-start.7
  120.0 0.7 convert_reduce_fusion.1.starts
  120.6 2.1 collective-permute-start.26
  122.7 0.6 pad_add_fusion.meta
  123.5 0.7 select_reduce_fusion.entries
  124.2 1.5 collective-permute-start.19
  125.8 2.3 %collective-permute-start.24 = (bf16[2272,256]{1,0:T(8,128)(2,1)}, bf16[2272,256]{1,0:T(8,128)(2,1)S(1)}, u32[]{:S(2)}, u32[]{:S(2)}) collective-permute-start(bf16[2272,256]{1,0:T(8,128)(2,1)} %collective-permute-done.21.refs_11_.refs_7_), channel_id=1, source_target_pairs={{0,96},{8,104},{16,112},{24,120},{32,0},{40,8},{48,16},{56,24},{64... | collective-permute-start | bytes 3489800 | tf_op jit(solution)/shard_map/ppermute | solution.py:519
  128.1 0.5 collective-permute-start.18
  128.6 0.6 copy-done.15
  129.2 1.1 copy-done.16
  130.2 21.8 %near.2 = (bf16[8,2048,256]{2,1,0:T(8,128)(2,1)}, f32[128,128]{1,0:T(8,128)}, f32[16,64,128]{2,1,0:T(8,128)}, f32[128,64,128]{2,1,0:T(8,128)}) custom-call(s32[2]{0:T(128)} %pad_add_fusion.meta, s32[16,16]{1,0:T(8,128)} %near.3, s32[4]{0:T(128)} %convert_reduce_fusion.1.starts, s32[384]{0:T(512)} %select_reduce_fusion.entries, ...), custom_call_target="tpu_custom_call" | custom-call | flops 8999999488 | bytes 30000000 | tf_op jit(solution)/shard_map/near/pallas_call | solution.py:359
  152.1 25.1 %shard_map.73.refs_10_ = f32[128,64,128]{2,1,0:T(8,128)} custom-call(s32[4]{0:T(128)} %convert_reduce_fusion.1.starts, s32[384]{0:T(512)} %select_reduce_fusion.entries, bf16[8,2048,256]{2,1,0:T(8,128)(2,1)} %get-tuple-element.18.x_hbm, f32[128,128]{1,0:T(8,128)} %get-tuple-element.19.norm_ref, ...), custom_call_target="tpu_custom_call" | custom-call | flops 10000000000 | bytes 25000000 | tf_op jit(solution)/shard_map/pallas_call | solution.py:474
  177.2 1.0 copy-done.3
  178.2 0.4 copy-done.4
  178.6 15.8 %shard_map.74 = (f32[64,64,128]{2,1,0:T(8,128)}, bf16[64,64,128]{2,1,0:T(8,128)(2,1)}) custom-call(s32[4]{0:T(128)} %convert_reduce_fusion.1.starts, s32[384]{0:T(512)} %select_reduce_fusion.entries, bf16[8,2048,256]{2,1,0:T(8,128)(2,1)} %get-tuple-element.18.x_hbm, f32[128,128]{1,0:T(8,128)} %get-tuple-element.19.norm_ref, bf16[2272,256]{1,0:T(8,128)(2,1)} %copy-done, ...), custom_call_target="tpu_custom_call" | custom-call | flops 5000000000 | bytes 25000000 | tf_op jit(solution)/shard_map/pallas_call | solution.py:474
  194.4 1.0 collective-permute-start.27
  195.4 2.5 %collective-permute-done.27 = bf16[64,64,128]{2,1,0:T(8,128)(2,1)S(1)} collective-permute-done((bf16[64,64,128]{2,1,0:T(8,128)(2,1)}, bf16[64,64,128]{2,1,0:T(8,128)(2,1)S(1)}, u32[]{:S(2)}, u32[]{:S(2)}) %collective-permute-start.27) | collective-permute-done | bytes 1048608 | tf_op jit(solution)/shard_map/ppermute | solution.py:519
  197.9 2.0 fusion.30
  199.9 4.1 %collective-permute-start.28 = (bf16[16,64,128]{2,1,0:T(8,128)(2,1)S(1)}, bf16[16,64,128]{2,1,0:T(8,128)(2,1)S(1)}, u32[]{:S(2)}, u32[]{:S(2)}) collective-permute-start(bf16[16,64,128]{2,1,0:T(8,128)(2,1)S(1)} %get-tuple-element.27), channel_id=1, source_target_pairs={{0,6},{1,7},{2,0},{3,1},{4,2},{5,3},{6,4},{7,5},{8,14},{9,15},{10,... | collective-permute-start | bytes 786440 | tf_op jit(solution)/shard_map/ppermute | solution.py:519
  204.0 1.5 collective-permute-start.30
  205.6 9.9 %collective-permute-done.28 = bf16[16,64,128]{2,1,0:T(8,128)(2,1)S(1)} collective-permute-done((bf16[16,64,128]{2,1,0:T(8,128)(2,1)S(1)}, bf16[16,64,128]{2,1,0:T(8,128)(2,1)S(1)}, u32[]{:S(2)}, u32[]{:S(2)}) %collective-permute-start.28) | collective-permute-done | bytes 262176 | tf_op jit(solution)/shard_map/ppermute | solution.py:519
  215.5 3.4 %collective-permute-done.29 = bf16[16,64,128]{2,1,0:T(8,128)(2,1)S(1)} collective-permute-done((bf16[16,64,128]{2,1,0:T(8,128)(2,1)S(1)}, bf16[16,64,128]{2,1,0:T(8,128)(2,1)S(1)}, u32[]{:S(2)}, u32[]{:S(2)}) %collective-permute-start.29) | collective-permute-done | bytes 262176 | tf_op jit(solution)/shard_map/ppermute | solution.py:519
  218.9 1.0 copy_bitcast_fusion
  (86 shorter events, 1.6 us)
Async XLA Ops:
  4.1 29.3 %collective-permute-start.10 = (bf16[1136,256]{1,0:T(8,128)(2,1)}, bf16[1136,256]{1,0:T(8,128)(2,1)S(1)}, u32[]{:S(2)}, u32[]{:S(2)}) collective-permute-start(bf16[1136,256]{1,0:T(8,128)(2,1)} %get-tuple-element.15), channel_id=1, source_target_pairs={{0,96},{8,104},{16,112},{24,120},{32,0},{40,8},{48,16},{56,24},{64... | collective-permute-start | bytes 1744904 | tf_op jit(solution)/shard_map/ppermute | solution.py:519
  8.3 26.8 %collective-permute-start.11 = (bf16[1136,256]{1,0:T(8,128)(2,1)}, bf16[1136,256]{1,0:T(8,128)(2,1)S(1)}, u32[]{:S(2)}, u32[]{:S(2)}) collective-permute-start(bf16[1136,256]{1,0:T(8,128)(2,1)} %get-tuple-element.15), channel_id=1, source_target_pairs={{0,64},{8,72},{16,80},{24,88},{32,96},{40,104},{48,112},{56,120},{... | collective-permute-start | bytes 1744904 | tf_op jit(solution)/shard_map/ppermute | solution.py:519
  8.3 26.8 %copy-start.13 = (bf16[2592,256]{1,0:T(8,128)(2,1)S(1)}, bf16[2592,256]{1,0:T(8,128)(2,1)}, u32[]{:S(2)}) copy-start(bf16[2592,256]{1,0:T(8,128)(2,1)} %get-tuple-element.14.refs_0_) | copy-start | bytes 3981316
  8.3 28.6 %collective-permute-start.13 = (bf16[1136,256]{1,0:T(8,128)(2,1)}, bf16[1136,256]{1,0:T(8,128)(2,1)S(1)}, u32[]{:S(2)}, u32[]{:S(2)}) collective-permute-start(bf16[1136,256]{1,0:T(8,128)(2,1)} %get-tuple-element.16), channel_id=1, source_target_pairs={{0,24},{8,0},{16,8},{24,16},{32,56},{40,32},{48,40},{56,48},{64,88... | collective-permute-start | bytes 1744904 | tf_op jit(solution)/shard_map/ppermute | solution.py:519
  11.0 25.9 %collective-permute-start.14 = (bf16[1136,256]{1,0:T(8,128)(2,1)}, bf16[1136,256]{1,0:T(8,128)(2,1)S(1)}, u32[]{:S(2)}, u32[]{:S(2)}) collective-permute-start(bf16[1136,256]{1,0:T(8,128)(2,1)} %get-tuple-element.16), channel_id=1, source_target_pairs={{0,16},{8,24},{16,0},{24,8},{32,48},{40,56},{48,32},{56,40},{64,80... | collective-permute-start | bytes 1744904 | tf_op jit(solution)/shard_map/ppermute | solution.py:519
  11.8 28.8 %collective-permute-start.9 = (bf16[1136,256]{1,0:T(8,128)(2,1)}, bf16[1136,256]{1,0:T(8,128)(2,1)S(1)}, u32[]{:S(2)}, u32[]{:S(2)}) collective-permute-start(bf16[1136,256]{1,0:T(8,128)(2,1)} %get-tuple-element.15), channel_id=1, source_target_pairs={{0,32},{8,40},{16,48},{24,56},{32,64},{40,72},{48,80},{56,88},{64,... | collective-permute-start | bytes 1744904 | tf_op jit(solution)/shard_map/ppermute | solution.py:519
  33.5 6.3 %copy-start.5 = (bf16[1136,256]{1,0:T(8,128)(2,1)S(1)}, bf16[1136,256]{1,0:T(8,128)(2,1)}, u32[]{:S(2)}) copy-start(bf16[1136,256]{1,0:T(8,128)(2,1)} %get-tuple-element.16) | copy-start | bytes 1744900
  33.5 31.4 %collective-permute-start = (bf16[2592,256]{1,0:T(8,128)(2,1)}, bf16[2592,256]{1,0:T(8,128)(2,1)S(1)}, u32[]{:S(2)}, u32[]{:S(2)}) collective-permute-start(bf16[2592,256]{1,0:T(8,128)(2,1)} %get-tuple-element.14.refs_0_), channel_id=1, source_target_pairs={{0,2},{1,3},{2,4},{3,5},{4,6},{5,7},{6,0},{7,1},{8,10},{9,11},{10,... | collective-permute-start | bytes 3981320 | tf_op jit(solution)/shard_map/ppermute | solution.py:519
  35.1 31.2 %collective-permute-start.1 = (bf16[2592,256]{1,0:T(8,128)(2,1)S(1)}, bf16[2592,256]{1,0:T(8,128)(2,1)S(1)}, u32[]{:S(2)}, u32[]{:S(2)}) collective-permute-start(bf16[2592,256]{1,0:T(8,128)(2,1)S(1)} %copy-done.13), channel_id=1, source_target_pairs={{0,6},{1,7},{2,0},{3,1},{4,2},{5,3},{6,4},{7,5},{8,14},{9,15},{10,... | collective-permute-start | bytes 3981320 | tf_op jit(solution)/shard_map/ppermute | solution.py:519
  36.8 29.6 %collective-permute-start.4 = (bf16[2592,256]{1,0:T(8,128)(2,1)S(1)}, bf16[2592,256]{1,0:T(8,128)(2,1)S(1)}, u32[]{:S(2)}, u32[]{:S(2)}) collective-permute-start(bf16[2592,256]{1,0:T(8,128)(2,1)S(1)} %copy-done.13), channel_id=1, source_target_pairs={{0,1},{1,0},{2,3},{3,2},{4,5},{5,4},{6,7},{7,6},{8,9},{9,8},{10,11... | collective-permute-start | bytes 3981320 | tf_op jit(solution)/shard_map/ppermute | solution.py:519
  36.9 27.9 %copy-start = (bf16[2272,256]{1,0:T(8,128)(2,1)}, bf16[2272,256]{1,0:T(8,128)(2,1)S(1)}, u32[]{:S(2)}) copy-start(bf16[2272,256]{1,0:T(8,128)(2,1)S(1)} %constant_dynamic-update-slice_fusion.2.refs_11_.refs_1_.refs_0_) | copy-start | bytes 3489796
  36.9 31.1 %collective-permute-start.16 = (bf16[2272,256]{1,0:T(8,128)(2,1)S(1)}, bf16[2272,256]{1,0:T(8,128)(2,1)S(1)}, u32[]{:S(2)}, u32[]{:S(2)}) collective-permute-start(bf16[2272,256]{1,0:T(8,128)(2,1)S(1)} %constant_dynamic-update-slice_fusion.2.refs_11_.refs_1_.refs_0_), channel_id=1, source_target_pairs={{0,24},{8,0},{16,8},{24,16},{32,56},{40,32},{48,40},{56,48},{64,88... | collective-permute-start | bytes 3489800 | tf_op jit(solution)/shard_map/ppermute | solution.py:519
  40.6 16.5 %collective-permute-start.12 = (bf16[1136,256]{1,0:T(8,128)(2,1)S(1)}, bf16[1136,256]{1,0:T(8,128)(2,1)S(1)}, u32[]{:S(2)}, u32[]{:S(2)}) collective-permute-start(bf16[1136,256]{1,0:T(8,128)(2,1)S(1)} %copy-done.5), channel_id=1, source_target_pairs={{0,8},{8,16},{16,24},{24,0},{32,40},{40,48},{48,56},{56,32},{64,72... | collective-permute-start | bytes 1744904 | tf_op jit(solution)/shard_map/ppermute | solution.py:519
  40.7 25.6 %copy-start.1 = (bf16[2272,256]{1,0:T(8,128)(2,1)}, bf16[2272,256]{1,0:T(8,128)(2,1)S(1)}, u32[]{:S(2)}) copy-start(bf16[2272,256]{1,0:T(8,128)(2,1)S(1)} %constant_dynamic-update-slice_fusion.6.refs_13_.refs_7_.refs_5_) | copy-start | bytes 3489796
  57.1 28.0 %collective-permute-start.21 = (bf16[2272,256]{1,0:T(8,128)(2,1)S(1)}, bf16[2272,256]{1,0:T(8,128)(2,1)}, u32[]{:S(2)}, u32[]{:S(2)}) collective-permute-start(bf16[2272,256]{1,0:T(8,128)(2,1)S(1)} %constant_dynamic-update-slice_fusion.6.refs_13_.refs_7_.refs_5_), channel_id=1, source_target_pairs={{0,96},{8,104},{16,112},{24,120},{32,0},{40,8},{48,16},{56,24},{64... | collective-permute-start | bytes 3489800 | tf_op jit(solution)/shard_map/ppermute | solution.py:519
  64.8 20.3 %copy-start.7 = (bf16[2592,256]{1,0:T(8,128)(2,1)}, bf16[2592,256]{1,0:T(8,128)(2,1)S(1)}, u32[]{:S(2)}) copy-start(bf16[2592,256]{1,0:T(8,128)(2,1)S(1)} %collective-permute-done.refs_1_) | copy-start | bytes 3981316
  64.8 29.8 %collective-permute-start.15 = (bf16[2272,256]{1,0:T(8,128)(2,1)S(1)}, bf16[2272,256]{1,0:T(8,128)(2,1)}, u32[]{:S(2)}, u32[]{:S(2)}) collective-permute-start(bf16[2272,256]{1,0:T(8,128)(2,1)S(1)} %constant_dynamic-update-slice_fusion.2.refs_11_.refs_1_.refs_0_), channel_id=1, source_target_pairs={{0,8},{8,16},{16,24},{24,0},{32,40},{40,48},{48,56},{56,32},{64,72... | collective-permute-start | bytes 3489800 | tf_op jit(solution)/shard_map/ppermute | solution.py:519
  66.3 18.8 %copy-start.9 = (bf16[2592,256]{1,0:T(8,128)(2,1)}, bf16[2592,256]{1,0:T(8,128)(2,1)S(1)}, u32[]{:S(2)}) copy-start(bf16[2592,256]{1,0:T(8,128)(2,1)S(1)} %collective-permute-done.1.refs_2_) | copy-start | bytes 3981316
  66.3 30.4 %collective-permute-start.20 = (bf16[2272,256]{1,0:T(8,128)(2,1)S(1)}, bf16[2272,256]{1,0:T(8,128)(2,1)}, u32[]{:S(2)}, u32[]{:S(2)}) collective-permute-start(bf16[2272,256]{1,0:T(8,128)(2,1)S(1)} %constant_dynamic-update-slice_fusion.6.refs_13_.refs_7_.refs_5_), channel_id=1, source_target_pairs={{0,32},{8,40},{16,48},{24,56},{32,64},{40,72},{48,80},{56,88},{64,... | collective-permute-start | bytes 3489800 | tf_op jit(solution)/shard_map/ppermute | solution.py:519
  66.4 18.7 %copy-start.14 = (bf16[2592,256]{1,0:T(8,128)(2,1)}, bf16[2592,256]{1,0:T(8,128)(2,1)S(1)}, u32[]{:S(2)}) copy-start(bf16[2592,256]{1,0:T(8,128)(2,1)S(1)} %collective-permute-done.4.refs_5_) | copy-start | bytes 3981316
  66.4 50.2 %collective-permute-start.17 = (bf16[2272,256]{1,0:T(8,128)(2,1)}, bf16[2272,256]{1,0:T(8,128)(2,1)}, u32[]{:S(2)}, u32[]{:S(2)}) collective-permute-start(bf16[2272,256]{1,0:T(8,128)(2,1)} %constant_dynamic-update-slice_fusion.refs_10_.refs_0_), channel_id=1, source_target_pairs={{0,8},{8,16},{16,24},{24,0},{32,40},{40,48},{48,56},{56,32},{64,72... | collective-permute-start | bytes 3489800 | tf_op jit(solution)/shard_map/ppermute | solution.py:519
  68.0 56.2 %copy-start.2 = (bf16[2272,256]{1,0:T(8,128)(2,1)}, bf16[2272,256]{1,0:T(8,128)(2,1)S(1)}, u32[]{:S(2)}) copy-start(bf16[2272,256]{1,0:T(8,128)(2,1)S(1)} %collective-permute-done.16.refs_5_.refs_2_) | copy-start | bytes 3489796
  68.0 51.0 %collective-permute-start.22 = (bf16[2272,256]{1,0:T(8,128)(2,1)}, bf16[2272,256]{1,0:T(8,128)(2,1)}, u32[]{:S(2)}, u32[]{:S(2)}) collective-permute-start(bf16[2272,256]{1,0:T(8,128)(2,1)} %constant_dynamic-update-slice_fusion.4.refs_12_.refs_6_), channel_id=1, source_target_pairs={{0,32},{8,40},{16,48},{24,56},{32,64},{40,72},{48,80},{56,88},{64,... | collective-permute-start | bytes 3489800 | tf_op jit(solution)/shard_map/ppermute | solution.py:519
  85.1 35.5 %collective-permute-start.25 = (bf16[2272,256]{1,0:T(8,128)(2,1)}, bf16[2272,256]{1,0:T(8,128)(2,1)}, u32[]{:S(2)}, u32[]{:S(2)}) collective-permute-start(bf16[2272,256]{1,0:T(8,128)(2,1)} %constant_dynamic-update-slice_fusion.refs_10_.refs_0_), channel_id=1, source_target_pairs={{0,24},{8,0},{16,8},{24,16},{32,56},{40,32},{48,40},{56,48},{64,88... | collective-permute-start | bytes 3489800 | tf_op jit(solution)/shard_map/ppermute | solution.py:519
  85.2 1.5 copy-start.10
  85.2 31.4 %copy-start.8 = (bf16[2592,256]{1,0:T(8,128)(2,1)S(1)}, bf16[2592,256]{1,0:T(8,128)(2,1)}, u32[]{:S(2)}) copy-start(bf16[2592,256]{1,0:T(8,128)(2,1)} %copy-done.7) | copy-start | bytes 3981316
  85.2 33.7 %copy-start.11 = (s32[128,3,1]{0,2,1:T(1,128)S(1)}, s32[128,3,1]{0,2,1:T(1,128)}, u32[]{:S(2)}) copy-start(s32[128,3,1]{0,2,1:T(1,128)} %param.10) | copy-start | bytes 4612
  85.2 33.8 %copy-start.12 = (s32[112]{0:T(128)S(1)}, s32[112]{0:T(128)}, u32[]{:S(2)}) copy-start(s32[112]{0:T(128)} %constant.94.clone) | copy-start | bytes 1348
  94.6 24.5 %collective-permute-start.2 = (bf16[1296,256]{1,0:T(8,128)(2,1)S(1)}, bf16[1296,256]{1,0:T(8,128)(2,1)S(1)}, u32[]{:S(2)}, u32[]{:S(2)}) collective-permute-start(bf16[1296,256]{1,0:T(8,128)(2,1)S(1)} %slice.31), channel_id=1, source_target_pairs={{0,2},{1,3},{2,4},{3,5},{4,6},{5,7},{6,0},{7,1},{8,10},{9,11},{10,... | collective-permute-start | bytes 1990664 | tf_op jit(solution)/shard_map/ppermute | solution.py:519
  96.7 23.1 %collective-permute-start.3 = (bf16[1296,256]{1,0:T(8,128)(2,1)S(1)}, bf16[1296,256]{1,0:T(8,128)(2,1)S(1)}, u32[]{:S(2)}, u32[]{:S(2)}) collective-permute-start(bf16[1296,256]{1,0:T(8,128)(2,1)S(1)} %slice.32), channel_id=1, source_target_pairs={{0,6},{1,7},{2,0},{3,1},{4,2},{5,3},{6,4},{7,5},{8,14},{9,15},{10,... | collective-permute-start | bytes 1990664 | tf_op jit(solution)/shard_map/ppermute | solution.py:519
  116.6 11.4 %collective-permute-start.5 = (bf16[2592,256]{1,0:T(8,128)(2,1)S(1)}, bf16[2592,256]{1,0:T(8,128)(2,1)S(1)}, u32[]{:S(2)}, u32[]{:S(2)}) collective-permute-start(bf16[2592,256]{1,0:T(8,128)(2,1)S(1)} %copy-done.8), channel_id=1, source_target_pairs={{0,1},{1,0},{2,3},{3,2},{4,5},{5,4},{6,7},{7,6},{8,9},{9,8},{10,11... | collective-permute-start | bytes 3981320 | tf_op jit(solution)/shard_map/ppermute | solution.py:519
  118.9 9.6 %collective-permute-start.6 = (bf16[2592,256]{1,0:T(8,128)(2,1)S(1)}, bf16[2592,256]{1,0:T(8,128)(2,1)S(1)}, u32[]{:S(2)}, u32[]{:S(2)}) collective-permute-start(bf16[2592,256]{1,0:T(8,128)(2,1)S(1)} %copy-done.10), channel_id=1, source_target_pairs={{0,1},{1,0},{2,3},{3,2},{4,5},{5,4},{6,7},{7,6},{8,9},{9,8},{10,11... | collective-permute-start | bytes 3981320 | tf_op jit(solution)/shard_map/ppermute | solution.py:519
  119.2 9.4 %copy-start.17 = (bf16[1296,256]{1,0:T(8,128)(2,1)}, bf16[1296,256]{1,0:T(8,128)(2,1)S(1)}, u32[]{:S(2)}) copy-start(bf16[1296,256]{1,0:T(8,128)(2,1)S(1)} %collective-permute-done.2.refs_3_) | copy-start | bytes 1990660
  119.2 5.0 %collective-permute-start.7 = (bf16[1296,256]{1,0:T(8,128)(2,1)S(1)}, bf16[1296,256]{1,0:T(8,128)(2,1)S(1)}, u32[]{:S(2)}, u32[]{:S(2)}) collective-permute-start(bf16[1296,256]{1,0:T(8,128)(2,1)S(1)} %collective-permute-done.2.refs_3_), channel_id=1, source_target_pairs={{0,1},{1,0},{2,3},{3,2},{4,5},{5,4},{6,7},{7,6},{8,9},{9,8},{10,11... | collective-permute-start | bytes 1990664 | tf_op jit(solution)/shard_map/ppermute | solution.py:519
  119.8 8.8 %copy-start.18 = (bf16[1296,256]{1,0:T(8,128)(2,1)}, bf16[1296,256]{1,0:T(8,128)(2,1)S(1)}, u32[]{:S(2)}) copy-start(bf16[1296,256]{1,0:T(8,128)(2,1)S(1)} %collective-permute-done.3.refs_4_) | copy-start | bytes 1990660
  119.8 6.0 %collective-permute-start.8 = (bf16[1296,256]{1,0:T(8,128)(2,1)S(1)}, bf16[1296,256]{1,0:T(8,128)(2,1)S(1)}, u32[]{:S(2)}, u32[]{:S(2)}) collective-permute-start(bf16[1296,256]{1,0:T(8,128)(2,1)S(1)} %collective-permute-done.3.refs_4_), channel_id=1, source_target_pairs={{0,1},{1,0},{2,3},{3,2},{4,5},{5,4},{6,7},{7,6},{8,9},{9,8},{10,11... | collective-permute-start | bytes 1990664 | tf_op jit(solution)/shard_map/ppermute | solution.py:519
  120.6 31.4 %collective-permute-start.26 = (bf16[2272,256]{1,0:T(8,128)(2,1)}, bf16[2272,256]{1,0:T(8,128)(2,1)}, u32[]{:S(2)}, u32[]{:S(2)}) collective-permute-start(bf16[2272,256]{1,0:T(8,128)(2,1)} %constant_dynamic-update-slice_fusion.4.refs_12_.refs_6_), channel_id=1, source_target_pairs={{0,96},{8,104},{16,112},{24,120},{32,0},{40,8},{48,16},{56,24},{64... | collective-permute-start | bytes 3489800 | tf_op jit(solution)/shard_map/ppermute | solution.py:519
  124.2 4.3 %copy-start.19 = (bf16[1296,256]{1,0:T(8,128)(2,1)}, bf16[1296,256]{1,0:T(8,128)(2,1)S(1)}, u32[]{:S(2)}) copy-start(bf16[1296,256]{1,0:T(8,128)(2,1)S(1)} %collective-permute-done.7.refs_8_) | copy-start | bytes 1990660
  124.2 52.9 %collective-permute-start.19 = (bf16[2272,256]{1,0:T(8,128)(2,1)S(1)}, bf16[2272,256]{1,0:T(8,128)(2,1)S(1)}, u32[]{:S(2)}, u32[]{:S(2)}) collective-permute-start(bf16[2272,256]{1,0:T(8,128)(2,1)S(1)} %collective-permute-done.16.refs_5_.refs_2_), channel_id=1, source_target_pairs={{0,24},{8,0},{16,8},{24,16},{32,56},{40,32},{48,40},{56,48},{64,88... | collective-permute-start | bytes 3489800 | tf_op jit(solution)/shard_map/ppermute | solution.py:519
  125.8 2.8 %copy-start.20 = (bf16[1296,256]{1,0:T(8,128)(2,1)}, bf16[1296,256]{1,0:T(8,128)(2,1)S(1)}, u32[]{:S(2)}) copy-start(bf16[1296,256]{1,0:T(8,128)(2,1)S(1)} %collective-permute-done.8.refs_9_) | copy-start | bytes 1990660
  125.8 51.4 %collective-permute-start.24 = (bf16[2272,256]{1,0:T(8,128)(2,1)}, bf16[2272,256]{1,0:T(8,128)(2,1)S(1)}, u32[]{:S(2)}, u32[]{:S(2)}) collective-permute-start(bf16[2272,256]{1,0:T(8,128)(2,1)} %collective-permute-done.21.refs_11_.refs_7_), channel_id=1, source_target_pairs={{0,96},{8,104},{16,112},{24,120},{32,0},{40,8},{48,16},{56,24},{64... | collective-permute-start | bytes 3489800 | tf_op jit(solution)/shard_map/ppermute | solution.py:519
  128.1 49.1 %collective-permute-start.18 = (bf16[2272,256]{1,0:T(8,128)(2,1)}, bf16[2272,256]{1,0:T(8,128)(2,1)}, u32[]{:S(2)}, u32[]{:S(2)}) collective-permute-start(bf16[2272,256]{1,0:T(8,128)(2,1)} %collective-permute-done.17.refs_2_), channel_id=1, source_target_pairs={{0,8},{8,16},{16,24},{24,0},{32,40},{40,48},{48,56},{56,32},{64,72... | collective-permute-start | bytes 3489800 | tf_op jit(solution)/shard_map/ppermute | solution.py:519
  130.2 47.0 %collective-permute-start.23 = (bf16[2272,256]{1,0:T(8,128)(2,1)}, bf16[2272,256]{1,0:T(8,128)(2,1)}, u32[]{:S(2)}, u32[]{:S(2)}) collective-permute-start(bf16[2272,256]{1,0:T(8,128)(2,1)} %collective-permute-done.22.refs_8_), channel_id=1, source_target_pairs={{0,32},{8,40},{16,48},{24,56},{32,64},{40,72},{48,80},{56,88},{64,... | collective-permute-start | bytes 3489800 | tf_op jit(solution)/shard_map/ppermute | solution.py:519
  194.4 3.5 %collective-permute-start.27 = (bf16[64,64,128]{2,1,0:T(8,128)(2,1)}, bf16[64,64,128]{2,1,0:T(8,128)(2,1)S(1)}, u32[]{:S(2)}, u32[]{:S(2)}) collective-permute-start(bf16[64,64,128]{2,1,0:T(8,128)(2,1)} %get-tuple-element.22), channel_id=1, source_target_pairs={{0,1},{1,0},{2,3},{3,2},{4,5},{5,4},{6,7},{7,6},{8,9},{9,8},{10,11... | collective-permute-start | bytes 3145736 | tf_op jit(solution)/shard_map/ppermute | solution.py:519
  199.9 19.1 %copy-start.6 = (f32[16,64,128]{2,1,0:T(8,128)S(1)}, f32[16,64,128]{2,1,0:T(8,128)}, u32[]{:S(2)}) copy-start(f32[16,64,128]{2,1,0:T(8,128)} %get-tuple-element.17) | copy-start | bytes 1572868
  199.9 15.6 %collective-permute-start.28 = (bf16[16,64,128]{2,1,0:T(8,128)(2,1)S(1)}, bf16[16,64,128]{2,1,0:T(8,128)(2,1)S(1)}, u32[]{:S(2)}, u32[]{:S(2)}) collective-permute-start(bf16[16,64,128]{2,1,0:T(8,128)(2,1)S(1)} %get-tuple-element.27), channel_id=1, source_target_pairs={{0,6},{1,7},{2,0},{3,1},{4,2},{5,3},{6,4},{7,5},{8,14},{9,15},{10,... | collective-permute-start | bytes 786440 | tf_op jit(solution)/shard_map/ppermute | solution.py:519
  204.0 14.9 %collective-permute-start.29 = (bf16[16,64,128]{2,1,0:T(8,128)(2,1)S(1)}, bf16[16,64,128]{2,1,0:T(8,128)(2,1)S(1)}, u32[]{:S(2)}, u32[]{:S(2)}) collective-permute-start(bf16[16,64,128]{2,1,0:T(8,128)(2,1)S(1)} %get-tuple-element.29), channel_id=1, source_target_pairs={{0,2},{1,3},{2,4},{3,5},{4,6},{5,7},{6,0},{7,1},{8,10},{9,11},{10,... | collective-permute-start | bytes 786440 | tf_op jit(solution)/shard_map/ppermute | solution.py:519
  204.0 14.9 %collective-permute-start.30 = (bf16[16,64,128]{2,1,0:T(8,128)(2,1)S(1)}, bf16[16,64,128]{2,1,0:T(8,128)(2,1)S(1)}, u32[]{:S(2)}, u32[]{:S(2)}) collective-permute-start(bf16[16,64,128]{2,1,0:T(8,128)(2,1)S(1)} %get-tuple-element.28), channel_id=1, source_target_pairs={{0,4},{1,5},{2,6},{3,7},{4,0},{5,1},{6,2},{7,3},{8,12},{9,13},{10,... | collective-permute-start | bytes 786440 | tf_op jit(solution)/shard_map/ppermute | solution.py:519
  (4 other events, 4.6 us)

commit v2 on v1

--- a/solution.py
+++ b/solution.py
@@ -299,12 +299,13 @@
         for k in range(8):
             for copy in (loads[k // 4 * 9 + k % 4 * 2 :])[: 3 if k % 4 == 3 else 2]:
                 copy.wait()
-            store(k).start()
 
             v = ws[pl.ds(k * WROWS + WROWS - 32, 32), :].astype(F32)
             norm_out[pl.ds(k * BLK_DEV, BLK_DEV), :] = v[0:16, 0:BLK] + v[0:16, BLK:E] + v[16:32, 0:BLK]
         for copy in panel_copies:
             copy.start()
+        for k in range(8):
+            store(k).start()
 
         def source(i, slot):
             v = near[i, slot]
@@ -413,7 +414,7 @@
         def x_copy(k):
             return pltpu.make_async_copy(x_hbm.at[k], xs.at[pl.ds(k * PTS, PTS), :], xsem.at[k])
 
-        for copy in panel_copies + [x_copy(k) for k in range(8)] + [acc_copy]:
+        for copy in panel_copies + [x_copy(0)]:
             copy.start()
 
         def clear(b, carry):
@@ -423,6 +424,8 @@
         lax.fori_loop(0, BLOCKS + 1, clear, 0)
         for copy in panel_copies:
             copy.wait()
+        for copy in [x_copy(k) for k in range(1, 8)] + [acc_copy]:
+            copy.start()
         panel_norms(group, parts, wide, node_norms)
 
         def arrive(done, upto):

time: 220 us -> 213 us (0.968)
  Pallas kernels: 66.8 us -> 59.2 us
    pallas_call x2, Pallas kernels: 40.9 us -> 35.3 us  [far_call(): pl.pallas_call(body, grid_spec=pltpu.PrefetchScalarGridSpec(num_scalar_pr...]
  transfers between devices with their start and end apart: 31 -> 31, of which waited for: 11 -> 12; matrix products, arithmetic and copies ran while one was open for 4% -> 4% of each run, Pallas kernels for 21% -> 20%
where the time goes in v2:
time: 213 us; the launch traced here: 212 us
  waiting for transfers between devices  101 us (47%)
  Pallas kernels  59.2 us (28%)
  starting transfers between devices  37 us (17%)
  local copies, waits for them, and re-layouts  9.07 us (4%)
  other arithmetic  5.42 us (3%)
    ppermute x31, waiting for transfers between devices, move(): return lax.ppermute(v, axis, pairs)  101 us
    ppermute x31, starting transfers between devices, move(): return lax.ppermute(v, axis, pairs)  37 us
    pallas_call x2, Pallas kernels, far_call(): pl.pallas_call(body, grid_spec=pltpu.PrefetchScalarGridSpec(num_scalar_pr...  35.3 us
    pallas_call x1, Pallas kernels, near_call(): pl.pallas_call(body, grid_spec=pltpu.PrefetchScalarGridSpec(num_scalar_pr...  19.8 us
    unnamed x46, local copies, waits for them, and re-layouts  5.84 us
  transfers between devices with their start and end apart: 31, of which 12 were waited for; matrix products, arithmetic and copies ran while one was open for 4% of the time, Pallas kernels for 20%

profile of v2, /device:TPU:0, one launch (start us, length us, event | category | flops | bytes accessed | tf_op | source)
XLA Modules:
  0.0 212.3 jit_solution(11035126046575354325)
XLA Ops:
  0.0 4.1 %prep.1 = (bf16[2592,256]{1,0:T(8,128)(2,1)}, bf16[1136,256]{1,0:T(8,128)(2,1)}, bf16[1136,256]{1,0:T(8,128)(2,1)}) custom-call(bf16[2048,256]{1,0:T(8,128)(2,1)} %pts.1, bf16[64,2048]{1,0:T(8,128)(2,1)} %bitcast.88, bf16[7,64,256]{2,1,0:T(8,128)(2,1)} %bitcast.89, s32[7,256]{1,0:T(8,128)} %idx.1), custom_call_target="tpu_custom_call" | custom-call | flops 1000000000 | bytes 8000000 | tf_op jit(solution)/shard_map/prep/pallas_call | solution.py:105
  4.1 4.1 %collective-permute-start.10 = (bf16[1136,256]{1,0:T(8,128)(2,1)}, bf16[1136,256]{1,0:T(8,128)(2,1)S(1)}, u32[]{:S(2)}, u32[]{:S(2)}) collective-permute-start(bf16[1136,256]{1,0:T(8,128)(2,1)} %get-tuple-element.15), channel_id=1, source_target_pairs={{0,96},{8,104},{16,112},{24,120},{32,0},{40,8},{48,16},{56,24},{64... | collective-permute-start | bytes 1744904 | tf_op jit(solution)/shard_map/ppermute | solution.py:522
  8.3 2.8 %collective-permute-start.13 = (bf16[1136,256]{1,0:T(8,128)(2,1)}, bf16[1136,256]{1,0:T(8,128)(2,1)S(1)}, u32[]{:S(2)}, u32[]{:S(2)}) collective-permute-start(bf16[1136,256]{1,0:T(8,128)(2,1)} %get-tuple-element.16), channel_id=1, source_target_pairs={{0,24},{8,0},{16,8},{24,16},{32,56},{40,32},{48,40},{56,48},{64,88... | collective-permute-start | bytes 1744904 | tf_op jit(solution)/shard_map/ppermute | solution.py:522
  11.0 0.8 collective-permute-start.14
  11.8 1.3 collective-permute-start.9
  13.1 2.0 constant_dynamic-update-slice_fusion.1
  15.1 18.4 %collective-permute-done.10 = bf16[1136,256]{1,0:T(8,128)(2,1)S(1)} collective-permute-done((bf16[1136,256]{1,0:T(8,128)(2,1)}, bf16[1136,256]{1,0:T(8,128)(2,1)S(1)}, u32[]{:S(2)}, u32[]{:S(2)}) %collective-permute-start.10) | collective-permute-done | bytes 581664 | tf_op jit(solution)/shard_map/ppermute | solution.py:522
  33.5 1.6 collective-permute-start
  35.1 1.7 collective-permute-start.1
  36.9 2.8 %collective-permute-start.16 = (bf16[2272,256]{1,0:T(8,128)(2,1)S(1)}, bf16[2272,256]{1,0:T(8,128)(2,1)S(1)}, u32[]{:S(2)}, u32[]{:S(2)}) collective-permute-start(bf16[2272,256]{1,0:T(8,128)(2,1)S(1)} %constant_dynamic-update-slice_fusion.2.refs_11_.refs_1_.refs_0_), channel_id=1, source_target_pairs={{0,24},{8,0},{16,8},{24,16},{32,56},{40,32},{48,40},{56,48},{64,88... | collective-permute-start | bytes 3489800 | tf_op jit(solution)/shard_map/ppermute | solution.py:522
  39.7 0.9 constant_dynamic-update-slice_fusion.5
  40.8 0.9 constant_dynamic-update-slice_fusion.refs_10_.refs_0_
  41.7 15.5 %collective-permute-done.12 = bf16[1136,256]{1,0:T(8,128)(2,1)S(1)} collective-permute-done((bf16[1136,256]{1,0:T(8,128)(2,1)S(1)}, bf16[1136,256]{1,0:T(8,128)(2,1)S(1)}, u32[]{:S(2)}, u32[]{:S(2)}) %collective-permute-start.12) | collective-permute-done | bytes 581664 | tf_op jit(solution)/shard_map/ppermute | solution.py:522
  57.1 3.6 %collective-permute-start.21 = (bf16[2272,256]{1,0:T(8,128)(2,1)S(1)}, bf16[2272,256]{1,0:T(8,128)(2,1)}, u32[]{:S(2)}, u32[]{:S(2)}) collective-permute-start(bf16[2272,256]{1,0:T(8,128)(2,1)S(1)} %constant_dynamic-update-slice_fusion.6.refs_13_.refs_7_.refs_5_), channel_id=1, source_target_pairs={{0,96},{8,104},{16,112},{24,120},{32,0},{40,8},{48,16},{56,24},{64... | collective-permute-start | bytes 3489800 | tf_op jit(solution)/shard_map/ppermute | solution.py:522
  60.7 0.9 constant_dynamic-update-slice_fusion.4.refs_12_.refs_6_
  61.6 3.2 %collective-permute-done.refs_1_ = bf16[2592,256]{1,0:T(8,128)(2,1)S(1)} collective-permute-done((bf16[2592,256]{1,0:T(8,128)(2,1)}, bf16[2592,256]{1,0:T(8,128)(2,1)S(1)}, u32[]{:S(2)}, u32[]{:S(2)}) %collective-permute-start) | collective-permute-done | bytes 1327136 | tf_op jit(solution)/shard_map/ppermute | solution.py:522
  64.8 1.5 collective-permute-start.15
  66.4 1.6 collective-permute-start.17
  68.0 17.1 %collective-permute-done.21.refs_11_.refs_7_ = bf16[2272,256]{1,0:T(8,128)(2,1)} collective-permute-done((bf16[2272,256]{1,0:T(8,128)(2,1)S(1)}, bf16[2272,256]{1,0:T(8,128)(2,1)}, u32[]{:S(2)}, u32[]{:S(2)}) %collective-permute-start.21) | collective-permute-done | bytes 1163296 | tf_op jit(solution)/shard_map/ppermute | solution.py:522
  85.3 1.3 slice.31
  86.8 7.9 %collective-permute-done.15.refs_3_.refs_1_ = bf16[2272,256]{1,0:T(8,128)(2,1)} collective-permute-done((bf16[2272,256]{1,0:T(8,128)(2,1)S(1)}, bf16[2272,256]{1,0:T(8,128)(2,1)}, u32[]{:S(2)}, u32[]{:S(2)}) %collective-permute-start.15) | collective-permute-done | bytes 1163296 | tf_op jit(solution)/shard_map/ppermute | solution.py:522
  94.6 0.3 collective-permute-start.2
  94.9 1.8 collective-permute-done.20.refs_9_.refs_6_
  96.7 1.7 collective-permute-start.3
  98.4 18.2 %collective-permute-done.17.refs_2_ = bf16[2272,256]{1,0:T(8,128)(2,1)} collective-permute-done((bf16[2272,256]{1,0:T(8,128)(2,1)}, bf16[2272,256]{1,0:T(8,128)(2,1)}, u32[]{:S(2)}, u32[]{:S(2)}) %collective-permute-start.17) | collective-permute-done | bytes 1163296 | tf_op jit(solution)/shard_map/ppermute | solution.py:522
  116.6 2.3 %collective-permute-done.22.refs_8_ = bf16[2272,256]{1,0:T(8,128)(2,1)} collective-permute-done((bf16[2272,256]{1,0:T(8,128)(2,1)}, bf16[2272,256]{1,0:T(8,128)(2,1)}, u32[]{:S(2)}, u32[]{:S(2)}) %collective-permute-start.22) | collective-permute-done | bytes 1163296 | tf_op jit(solution)/shard_map/ppermute | solution.py:522
  119.2 0.6 collective-permute-start.7
  120.0 0.7 convert_reduce_fusion.1.starts
  120.6 2.1 collective-permute-start.26
  122.7 0.6 pad_add_fusion.meta
  123.5 0.7 select_reduce_fusion.entries
  124.2 1.5 collective-permute-start.19
  125.8 2.3 %collective-permute-start.24 = (bf16[2272,256]{1,0:T(8,128)(2,1)}, bf16[2272,256]{1,0:T(8,128)(2,1)S(1)}, u32[]{:S(2)}, u32[]{:S(2)}) collective-permute-start(bf16[2272,256]{1,0:T(8,128)(2,1)} %collective-permute-done.21.refs_11_.refs_7_), channel_id=1, source_target_pairs={{0,96},{8,104},{16,112},{24,120},{32,0},{40,8},{48,16},{56,24},{64... | collective-permute-start | bytes 3489800 | tf_op jit(solution)/shard_map/ppermute | solution.py:522
  128.1 0.5 collective-permute-start.18
  128.6 0.6 copy-done.15
  129.2 1.1 copy-done.16
  130.2 19.8 %near.2 = (bf16[8,2048,256]{2,1,0:T(8,128)(2,1)}, f32[128,128]{1,0:T(8,128)}, f32[16,64,128]{2,1,0:T(8,128)}, f32[128,64,128]{2,1,0:T(8,128)}) custom-call(s32[2]{0:T(128)} %pad_add_fusion.meta, s32[16,16]{1,0:T(8,128)} %near.3, s32[4]{0:T(128)} %convert_reduce_fusion.1.starts, s32[384]{0:T(512)} %select_reduce_fusion.entries, ...), custom_call_target="tpu_custom_call" | custom-call | flops 8999999488 | bytes 30000000 | tf_op jit(solution)/shard_map/near/pallas_call | solution.py:360
  150.0 21.9 %shard_map.73.refs_10_ = f32[128,64,128]{2,1,0:T(8,128)} custom-call(s32[4]{0:T(128)} %convert_reduce_fusion.1.starts, s32[384]{0:T(512)} %select_reduce_fusion.entries, bf16[8,2048,256]{2,1,0:T(8,128)(2,1)} %get-tuple-element.18.x_hbm, f32[128,128]{1,0:T(8,128)} %get-tuple-element.19.norm_ref, ...), custom_call_target="tpu_custom_call" | custom-call | flops 10000000000 | bytes 25000000 | tf_op jit(solution)/shard_map/pallas_call | solution.py:477
  172.0 1.7 collective-permute-done.24.refs_9_
  173.7 1.0 copy-done.4
  174.7 13.4 %shard_map.74 = (f32[64,64,128]{2,1,0:T(8,128)}, bf16[64,64,128]{2,1,0:T(8,128)(2,1)}) custom-call(s32[4]{0:T(128)} %convert_reduce_fusion.1.starts, s32[384]{0:T(512)} %select_reduce_fusion.entries, bf16[8,2048,256]{2,1,0:T(8,128)(2,1)} %get-tuple-element.18.x_hbm, f32[128,128]{1,0:T(8,128)} %get-tuple-element.19.norm_ref, bf16[2272,256]{1,0:T(8,128)(2,1)} %copy-done, ...), custom_call_target="tpu_custom_call" | custom-call | flops 5000000000 | bytes 25000000 | tf_op jit(solution)/shard_map/pallas_call | solution.py:477
  188.3 2.9 %collective-permute-done.27 = bf16[64,64,128]{2,1,0:T(8,128)(2,1)S(1)} collective-permute-done((bf16[64,64,128]{2,1,0:T(8,128)(2,1)}, bf16[64,64,128]{2,1,0:T(8,128)(2,1)S(1)}, u32[]{:S(2)}, u32[]{:S(2)}) %collective-permute-start.27) | collective-permute-done | bytes 1048608 | tf_op jit(solution)/shard_map/ppermute | solution.py:522
  191.1 2.0 fusion.30
  193.2 3.2 %collective-permute-start.28 = (bf16[16,64,128]{2,1,0:T(8,128)(2,1)S(1)}, bf16[16,64,128]{2,1,0:T(8,128)(2,1)S(1)}, u32[]{:S(2)}, u32[]{:S(2)}) collective-permute-start(bf16[16,64,128]{2,1,0:T(8,128)(2,1)S(1)} %get-tuple-element.27), channel_id=1, source_target_pairs={{0,6},{1,7},{2,0},{3,1},{4,2},{5,3},{6,4},{7,5},{8,14},{9,15},{10,... | collective-permute-start | bytes 786440 | tf_op jit(solution)/shard_map/ppermute | solution.py:522
  196.4 2.7 %collective-permute-start.30 = (bf16[16,64,128]{2,1,0:T(8,128)(2,1)S(1)}, bf16[16,64,128]{2,1,0:T(8,128)(2,1)S(1)}, u32[]{:S(2)}, u32[]{:S(2)}) collective-permute-start(bf16[16,64,128]{2,1,0:T(8,128)(2,1)S(1)} %get-tuple-element.28), channel_id=1, source_target_pairs={{0,4},{1,5},{2,6},{3,7},{4,0},{5,1},{6,2},{7,3},{8,12},{9,13},{10,... | collective-permute-start | bytes 786440 | tf_op jit(solution)/shard_map/ppermute | solution.py:522
  199.1 8.8 %collective-permute-done.28 = bf16[16,64,128]{2,1,0:T(8,128)(2,1)S(1)} collective-permute-done((bf16[16,64,128]{2,1,0:T(8,128)(2,1)S(1)}, bf16[16,64,128]{2,1,0:T(8,128)(2,1)S(1)}, u32[]{:S(2)}, u32[]{:S(2)}) %collective-permute-start.28) | collective-permute-done | bytes 262176 | tf_op jit(solution)/shard_map/ppermute | solution.py:522
  207.9 3.4 %collective-permute-done.29 = bf16[16,64,128]{2,1,0:T(8,128)(2,1)S(1)} collective-permute-done((bf16[16,64,128]{2,1,0:T(8,128)(2,1)S(1)}, bf16[16,64,128]{2,1,0:T(8,128)(2,1)S(1)}, u32[]{:S(2)}, u32[]{:S(2)}) %collective-permute-start.29) | collective-permute-done | bytes 262176 | tf_op jit(solution)/shard_map/ppermute | solution.py:522
  211.3 1.0 copy_bitcast_fusion
  (86 shorter events, 1.4 us)
Async XLA Ops:
  4.1 29.3 %collective-permute-start.10 = (bf16[1136,256]{1,0:T(8,128)(2,1)}, bf16[1136,256]{1,0:T(8,128)(2,1)S(1)}, u32[]{:S(2)}, u32[]{:S(2)}) collective-permute-start(bf16[1136,256]{1,0:T(8,128)(2,1)} %get-tuple-element.15), channel_id=1, source_target_pairs={{0,96},{8,104},{16,112},{24,120},{32,0},{40,8},{48,16},{56,24},{64... | collective-permute-start | bytes 1744904 | tf_op jit(solution)/shard_map/ppermute | solution.py:522
  8.3 26.8 %collective-permute-start.11 = (bf16[1136,256]{1,0:T(8,128)(2,1)}, bf16[1136,256]{1,0:T(8,128)(2,1)S(1)}, u32[]{:S(2)}, u32[]{:S(2)}) collective-permute-start(bf16[1136,256]{1,0:T(8,128)(2,1)} %get-tuple-element.15), channel_id=1, source_target_pairs={{0,64},{8,72},{16,80},{24,88},{32,96},{40,104},{48,112},{56,120},{... | collective-permute-start | bytes 1744904 | tf_op jit(solution)/shard_map/ppermute | solution.py:522
  8.3 26.8 %copy-start.13 = (bf16[2592,256]{1,0:T(8,128)(2,1)S(1)}, bf16[2592,256]{1,0:T(8,128)(2,1)}, u32[]{:S(2)}) copy-start(bf16[2592,256]{1,0:T(8,128)(2,1)} %get-tuple-element.14.refs_0_) | copy-start | bytes 3981316
  8.3 28.6 %collective-permute-start.13 = (bf16[1136,256]{1,0:T(8,128)(2,1)}, bf16[1136,256]{1,0:T(8,128)(2,1)S(1)}, u32[]{:S(2)}, u32[]{:S(2)}) collective-permute-start(bf16[1136,256]{1,0:T(8,128)(2,1)} %get-tuple-element.16), channel_id=1, source_target_pairs={{0,24},{8,0},{16,8},{24,16},{32,56},{40,32},{48,40},{56,48},{64,88... | collective-permute-start | bytes 1744904 | tf_op jit(solution)/shard_map/ppermute | solution.py:522
  11.0 25.9 %collective-permute-start.14 = (bf16[1136,256]{1,0:T(8,128)(2,1)}, bf16[1136,256]{1,0:T(8,128)(2,1)S(1)}, u32[]{:S(2)}, u32[]{:S(2)}) collective-permute-start(bf16[1136,256]{1,0:T(8,128)(2,1)} %get-tuple-element.16), channel_id=1, source_target_pairs={{0,16},{8,24},{16,0},{24,8},{32,48},{40,56},{48,32},{56,40},{64,80... | collective-permute-start | bytes 1744904 | tf_op jit(solution)/shard_map/ppermute | solution.py:522
  11.8 28.8 %collective-permute-start.9 = (bf16[1136,256]{1,0:T(8,128)(2,1)}, bf16[1136,256]{1,0:T(8,128)(2,1)S(1)}, u32[]{:S(2)}, u32[]{:S(2)}) collective-permute-start(bf16[1136,256]{1,0:T(8,128)(2,1)} %get-tuple-element.15), channel_id=1, source_target_pairs={{0,32},{8,40},{16,48},{24,56},{32,64},{40,72},{48,80},{56,88},{64,... | collective-permute-start | bytes 1744904 | tf_op jit(solution)/shard_map/ppermute | solution.py:522
  33.5 6.3 %copy-start.5 = (bf16[1136,256]{1,0:T(8,128)(2,1)S(1)}, bf16[1136,256]{1,0:T(8,128)(2,1)}, u32[]{:S(2)}) copy-start(bf16[1136,256]{1,0:T(8,128)(2,1)} %get-tuple-element.16) | copy-start | bytes 1744900
  33.5 31.4 %collective-permute-start = (bf16[2592,256]{1,0:T(8,128)(2,1)}, bf16[2592,256]{1,0:T(8,128)(2,1)S(1)}, u32[]{:S(2)}, u32[]{:S(2)}) collective-permute-start(bf16[2592,256]{1,0:T(8,128)(2,1)} %get-tuple-element.14.refs_0_), channel_id=1, source_target_pairs={{0,2},{1,3},{2,4},{3,5},{4,6},{5,7},{6,0},{7,1},{8,10},{9,11},{10,... | collective-permute-start | bytes 3981320 | tf_op jit(solution)/shard_map/ppermute | solution.py:522
  35.1 31.2 %collective-permute-start.1 = (bf16[2592,256]{1,0:T(8,128)(2,1)S(1)}, bf16[2592,256]{1,0:T(8,128)(2,1)S(1)}, u32[]{:S(2)}, u32[]{:S(2)}) collective-permute-start(bf16[2592,256]{1,0:T(8,128)(2,1)S(1)} %copy-done.13), channel_id=1, source_target_pairs={{0,6},{1,7},{2,0},{3,1},{4,2},{5,3},{6,4},{7,5},{8,14},{9,15},{10,... | collective-permute-start | bytes 3981320 | tf_op jit(solution)/shard_map/ppermute | solution.py:522
  36.8 29.6 %collective-permute-start.4 = (bf16[2592,256]{1,0:T(8,128)(2,1)S(1)}, bf16[2592,256]{1,0:T(8,128)(2,1)S(1)}, u32[]{:S(2)}, u32[]{:S(2)}) collective-permute-start(bf16[2592,256]{1,0:T(8,128)(2,1)S(1)} %copy-done.13), channel_id=1, source_target_pairs={{0,1},{1,0},{2,3},{3,2},{4,5},{5,4},{6,7},{7,6},{8,9},{9,8},{10,11... | collective-permute-start | bytes 3981320 | tf_op jit(solution)/shard_map/ppermute | solution.py:522
  36.9 27.9 %copy-start = (bf16[2272,256]{1,0:T(8,128)(2,1)}, bf16[2272,256]{1,0:T(8,128)(2,1)S(1)}, u32[]{:S(2)}) copy-start(bf16[2272,256]{1,0:T(8,128)(2,1)S(1)} %constant_dynamic-update-slice_fusion.2.refs_11_.refs_1_.refs_0_) | copy-start | bytes 3489796
  36.9 31.1 %collective-permute-start.16 = (bf16[2272,256]{1,0:T(8,128)(2,1)S(1)}, bf16[2272,256]{1,0:T(8,128)(2,1)S(1)}, u32[]{:S(2)}, u32[]{:S(2)}) collective-permute-start(bf16[2272,256]{1,0:T(8,128)(2,1)S(1)} %constant_dynamic-update-slice_fusion.2.refs_11_.refs_1_.refs_0_), channel_id=1, source_target_pairs={{0,24},{8,0},{16,8},{24,16},{32,56},{40,32},{48,40},{56,48},{64,88... | collective-permute-start | bytes 3489800 | tf_op jit(solution)/shard_map/ppermute | solution.py:522
  40.6 16.5 %collective-permute-start.12 = (bf16[1136,256]{1,0:T(8,128)(2,1)S(1)}, bf16[1136,256]{1,0:T(8,128)(2,1)S(1)}, u32[]{:S(2)}, u32[]{:S(2)}) collective-permute-start(bf16[1136,256]{1,0:T(8,128)(2,1)S(1)} %copy-done.5), channel_id=1, source_target_pairs={{0,8},{8,16},{16,24},{24,0},{32,40},{40,48},{48,56},{56,32},{64,72... | collective-permute-start | bytes 1744904 | tf_op jit(solution)/shard_map/ppermute | solution.py:522
  40.7 25.6 %copy-start.1 = (bf16[2272,256]{1,0:T(8,128)(2,1)}, bf16[2272,256]{1,0:T(8,128)(2,1)S(1)}, u32[]{:S(2)}) copy-start(bf16[2272,256]{1,0:T(8,128)(2,1)S(1)} %constant_dynamic-update-slice_fusion.6.refs_13_.refs_7_.refs_5_) | copy-start | bytes 3489796
  57.1 28.0 %collective-permute-start.21 = (bf16[2272,256]{1,0:T(8,128)(2,1)S(1)}, bf16[2272,256]{1,0:T(8,128)(2,1)}, u32[]{:S(2)}, u32[]{:S(2)}) collective-permute-start(bf16[2272,256]{1,0:T(8,128)(2,1)S(1)} %constant_dynamic-update-slice_fusion.6.refs_13_.refs_7_.refs_5_), channel_id=1, source_target_pairs={{0,96},{8,104},{16,112},{24,120},{32,0},{40,8},{48,16},{56,24},{64... | collective-permute-start | bytes 3489800 | tf_op jit(solution)/shard_map/ppermute | solution.py:522
  64.8 20.3 %copy-start.7 = (bf16[2592,256]{1,0:T(8,128)(2,1)}, bf16[2592,256]{1,0:T(8,128)(2,1)S(1)}, u32[]{:S(2)}) copy-start(bf16[2592,256]{1,0:T(8,128)(2,1)S(1)} %collective-permute-done.refs_1_) | copy-start | bytes 3981316
  64.8 29.8 %collective-permute-start.15 = (bf16[2272,256]{1,0:T(8,128)(2,1)S(1)}, bf16[2272,256]{1,0:T(8,128)(2,1)}, u32[]{:S(2)}, u32[]{:S(2)}) collective-permute-start(bf16[2272,256]{1,0:T(8,128)(2,1)S(1)} %constant_dynamic-update-slice_fusion.2.refs_11_.refs_1_.refs_0_), channel_id=1, source_target_pairs={{0,8},{8,16},{16,24},{24,0},{32,40},{40,48},{48,56},{56,32},{64,72... | collective-permute-start | bytes 3489800 | tf_op jit(solution)/shard_map/ppermute | solution.py:522
  66.3 18.8 %copy-start.9 = (bf16[2592,256]{1,0:T(8,128)(2,1)}, bf16[2592,256]{1,0:T(8,128)(2,1)S(1)}, u32[]{:S(2)}) copy-start(bf16[2592,256]{1,0:T(8,128)(2,1)S(1)} %collective-permute-done.1.refs_2_) | copy-start | bytes 3981316
  66.3 30.4 %collective-permute-start.20 = (bf16[2272,256]{1,0:T(8,128)(2,1)S(1)}, bf16[2272,256]{1,0:T(8,128)(2,1)}, u32[]{:S(2)}, u32[]{:S(2)}) collective-permute-start(bf16[2272,256]{1,0:T(8,128)(2,1)S(1)} %constant_dynamic-update-slice_fusion.6.refs_13_.refs_7_.refs_5_), channel_id=1, source_target_pairs={{0,32},{8,40},{16,48},{24,56},{32,64},{40,72},{48,80},{56,88},{64,... | collective-permute-start | bytes 3489800 | tf_op jit(solution)/shard_map/ppermute | solution.py:522
  66.4 18.7 %copy-start.14 = (bf16[2592,256]{1,0:T(8,128)(2,1)}, bf16[2592,256]{1,0:T(8,128)(2,1)S(1)}, u32[]{:S(2)}) copy-start(bf16[2592,256]{1,0:T(8,128)(2,1)S(1)} %collective-permute-done.4.refs_5_) | copy-start | bytes 3981316
  66.4 50.2 %collective-permute-start.17 = (bf16[2272,256]{1,0:T(8,128)(2,1)}, bf16[2272,256]{1,0:T(8,128)(2,1)}, u32[]{:S(2)}, u32[]{:S(2)}) collective-permute-start(bf16[2272,256]{1,0:T(8,128)(2,1)} %constant_dynamic-update-slice_fusion.refs_10_.refs_0_), channel_id=1, source_target_pairs={{0,8},{8,16},{16,24},{24,0},{32,40},{40,48},{48,56},{56,32},{64,72... | collective-permute-start | bytes 3489800 | tf_op jit(solution)/shard_map/ppermute | solution.py:522
  68.0 56.2 %copy-start.2 = (bf16[2272,256]{1,0:T(8,128)(2,1)}, bf16[2272,256]{1,0:T(8,128)(2,1)S(1)}, u32[]{:S(2)}) copy-start(bf16[2272,256]{1,0:T(8,128)(2,1)S(1)} %collective-permute-done.16.refs_5_.refs_2_) | copy-start | bytes 3489796
  68.0 51.0 %collective-permute-start.22 = (bf16[2272,256]{1,0:T(8,128)(2,1)}, bf16[2272,256]{1,0:T(8,128)(2,1)}, u32[]{:S(2)}, u32[]{:S(2)}) collective-permute-start(bf16[2272,256]{1,0:T(8,128)(2,1)} %constant_dynamic-update-slice_fusion.4.refs_12_.refs_6_), channel_id=1, source_target_pairs={{0,32},{8,40},{16,48},{24,56},{32,64},{40,72},{48,80},{56,88},{64,... | collective-permute-start | bytes 3489800 | tf_op jit(solution)/shard_map/ppermute | solution.py:522
  85.1 35.5 %collective-permute-start.25 = (bf16[2272,256]{1,0:T(8,128)(2,1)}, bf16[2272,256]{1,0:T(8,128)(2,1)}, u32[]{:S(2)}, u32[]{:S(2)}) collective-permute-start(bf16[2272,256]{1,0:T(8,128)(2,1)} %constant_dynamic-update-slice_fusion.refs_10_.refs_0_), channel_id=1, source_target_pairs={{0,24},{8,0},{16,8},{24,16},{32,56},{40,32},{48,40},{56,48},{64,88... | collective-permute-start | bytes 3489800 | tf_op jit(solution)/shard_map/ppermute | solution.py:522
  85.2 31.4 %copy-start.8 = (bf16[2592,256]{1,0:T(8,128)(2,1)S(1)}, bf16[2592,256]{1,0:T(8,128)(2,1)}, u32[]{:S(2)}) copy-start(bf16[2592,256]{1,0:T(8,128)(2,1)} %copy-done.7) | copy-start | bytes 3981316
  85.2 33.7 %copy-start.11 = (s32[128,3,1]{0,2,1:T(1,128)S(1)}, s32[128,3,1]{0,2,1:T(1,128)}, u32[]{:S(2)}) copy-start(s32[128,3,1]{0,2,1:T(1,128)} %param.10) | copy-start | bytes 4612
  85.2 33.8 %copy-start.12 = (s32[112]{0:T(128)S(1)}, s32[112]{0:T(128)}, u32[]{:S(2)}) copy-start(s32[112]{0:T(128)} %constant.94.clone) | copy-start | bytes 1348
  94.6 24.5 %collective-permute-start.2 = (bf16[1296,256]{1,0:T(8,128)(2,1)S(1)}, bf16[1296,256]{1,0:T(8,128)(2,1)S(1)}, u32[]{:S(2)}, u32[]{:S(2)}) collective-permute-start(bf16[1296,256]{1,0:T(8,128)(2,1)S(1)} %slice.31), channel_id=1, source_target_pairs={{0,2},{1,3},{2,4},{3,5},{4,6},{5,7},{6,0},{7,1},{8,10},{9,11},{10,... | collective-permute-start | bytes 1990664 | tf_op jit(solution)/shard_map/ppermute | solution.py:522
  96.7 23.1 %collective-permute-start.3 = (bf16[1296,256]{1,0:T(8,128)(2,1)S(1)}, bf16[1296,256]{1,0:T(8,128)(2,1)S(1)}, u32[]{:S(2)}, u32[]{:S(2)}) collective-permute-start(bf16[1296,256]{1,0:T(8,128)(2,1)S(1)} %slice.32), channel_id=1, source_target_pairs={{0,6},{1,7},{2,0},{3,1},{4,2},{5,3},{6,4},{7,5},{8,14},{9,15},{10,... | collective-permute-start | bytes 1990664 | tf_op jit(solution)/shard_map/ppermute | solution.py:522
  116.6 11.4 %collective-permute-start.5 = (bf16[2592,256]{1,0:T(8,128)(2,1)S(1)}, bf16[2592,256]{1,0:T(8,128)(2,1)S(1)}, u32[]{:S(2)}, u32[]{:S(2)}) collective-permute-start(bf16[2592,256]{1,0:T(8,128)(2,1)S(1)} %copy-done.8), channel_id=1, source_target_pairs={{0,1},{1,0},{2,3},{3,2},{4,5},{5,4},{6,7},{7,6},{8,9},{9,8},{10,11... | collective-permute-start | bytes 3981320 | tf_op jit(solution)/shard_map/ppermute | solution.py:522
  118.9 9.6 %collective-permute-start.6 = (bf16[2592,256]{1,0:T(8,128)(2,1)S(1)}, bf16[2592,256]{1,0:T(8,128)(2,1)S(1)}, u32[]{:S(2)}, u32[]{:S(2)}) collective-permute-start(bf16[2592,256]{1,0:T(8,128)(2,1)S(1)} %copy-done.10), channel_id=1, source_target_pairs={{0,1},{1,0},{2,3},{3,2},{4,5},{5,4},{6,7},{7,6},{8,9},{9,8},{10,11... | collective-permute-start | bytes 3981320 | tf_op jit(solution)/shard_map/ppermute | solution.py:522
  119.2 9.4 %copy-start.17 = (bf16[1296,256]{1,0:T(8,128)(2,1)}, bf16[1296,256]{1,0:T(8,128)(2,1)S(1)}, u32[]{:S(2)}) copy-start(bf16[1296,256]{1,0:T(8,128)(2,1)S(1)} %collective-permute-done.2.refs_3_) | copy-start | bytes 1990660
  119.2 5.0 %collective-permute-start.7 = (bf16[1296,256]{1,0:T(8,128)(2,1)S(1)}, bf16[1296,256]{1,0:T(8,128)(2,1)S(1)}, u32[]{:S(2)}, u32[]{:S(2)}) collective-permute-start(bf16[1296,256]{1,0:T(8,128)(2,1)S(1)} %collective-permute-done.2.refs_3_), channel_id=1, source_target_pairs={{0,1},{1,0},{2,3},{3,2},{4,5},{5,4},{6,7},{7,6},{8,9},{9,8},{10,11... | collective-permute-start | bytes 1990664 | tf_op jit(solution)/shard_map/ppermute | solution.py:522
  119.8 8.8 %copy-start.18 = (bf16[1296,256]{1,0:T(8,128)(2,1)}, bf16[1296,256]{1,0:T(8,128)(2,1)S(1)}, u32[]{:S(2)}) copy-start(bf16[1296,256]{1,0:T(8,128)(2,1)S(1)} %collective-permute-done.3.refs_4_) | copy-start | bytes 1990660
  119.8 6.0 %collective-permute-start.8 = (bf16[1296,256]{1,0:T(8,128)(2,1)S(1)}, bf16[1296,256]{1,0:T(8,128)(2,1)S(1)}, u32[]{:S(2)}, u32[]{:S(2)}) collective-permute-start(bf16[1296,256]{1,0:T(8,128)(2,1)S(1)} %collective-permute-done.3.refs_4_), channel_id=1, source_target_pairs={{0,1},{1,0},{2,3},{3,2},{4,5},{5,4},{6,7},{7,6},{8,9},{9,8},{10,11... | collective-permute-start | bytes 1990664 | tf_op jit(solution)/shard_map/ppermute | solution.py:522
  120.6 29.4 %collective-permute-start.26 = (bf16[2272,256]{1,0:T(8,128)(2,1)}, bf16[2272,256]{1,0:T(8,128)(2,1)}, u32[]{:S(2)}, u32[]{:S(2)}) collective-permute-start(bf16[2272,256]{1,0:T(8,128)(2,1)} %constant_dynamic-update-slice_fusion.4.refs_12_.refs_6_), channel_id=1, source_target_pairs={{0,96},{8,104},{16,112},{24,120},{32,0},{40,8},{48,16},{56,24},{64... | collective-permute-start | bytes 3489800 | tf_op jit(solution)/shard_map/ppermute | solution.py:522
  124.2 4.3 %copy-start.19 = (bf16[1296,256]{1,0:T(8,128)(2,1)}, bf16[1296,256]{1,0:T(8,128)(2,1)S(1)}, u32[]{:S(2)}) copy-start(bf16[1296,256]{1,0:T(8,128)(2,1)S(1)} %collective-permute-done.7.refs_8_) | copy-start | bytes 1990660
  124.2 47.7 %collective-permute-start.19 = (bf16[2272,256]{1,0:T(8,128)(2,1)S(1)}, bf16[2272,256]{1,0:T(8,128)(2,1)S(1)}, u32[]{:S(2)}, u32[]{:S(2)}) collective-permute-start(bf16[2272,256]{1,0:T(8,128)(2,1)S(1)} %collective-permute-done.16.refs_5_.refs_2_), channel_id=1, source_target_pairs={{0,24},{8,0},{16,8},{24,16},{32,56},{40,32},{48,40},{56,48},{64,88... | collective-permute-start | bytes 3489800 | tf_op jit(solution)/shard_map/ppermute | solution.py:522
  125.8 2.8 %copy-start.20 = (bf16[1296,256]{1,0:T(8,128)(2,1)}, bf16[1296,256]{1,0:T(8,128)(2,1)S(1)}, u32[]{:S(2)}) copy-start(bf16[1296,256]{1,0:T(8,128)(2,1)S(1)} %collective-permute-done.8.refs_9_) | copy-start | bytes 1990660
  125.8 47.9 %collective-permute-start.24 = (bf16[2272,256]{1,0:T(8,128)(2,1)}, bf16[2272,256]{1,0:T(8,128)(2,1)S(1)}, u32[]{:S(2)}, u32[]{:S(2)}) collective-permute-start(bf16[2272,256]{1,0:T(8,128)(2,1)} %collective-permute-done.21.refs_11_.refs_7_), channel_id=1, source_target_pairs={{0,96},{8,104},{16,112},{24,120},{32,0},{40,8},{48,16},{56,24},{64... | collective-permute-start | bytes 3489800 | tf_op jit(solution)/shard_map/ppermute | solution.py:522
  128.1 45.6 %collective-permute-start.18 = (bf16[2272,256]{1,0:T(8,128)(2,1)}, bf16[2272,256]{1,0:T(8,128)(2,1)}, u32[]{:S(2)}, u32[]{:S(2)}) collective-permute-start(bf16[2272,256]{1,0:T(8,128)(2,1)} %collective-permute-done.17.refs_2_), channel_id=1, source_target_pairs={{0,8},{8,16},{16,24},{24,0},{32,40},{40,48},{48,56},{56,32},{64,72... | collective-permute-start | bytes 3489800 | tf_op jit(solution)/shard_map/ppermute | solution.py:522
  130.2 43.5 %collective-permute-start.23 = (bf16[2272,256]{1,0:T(8,128)(2,1)}, bf16[2272,256]{1,0:T(8,128)(2,1)}, u32[]{:S(2)}, u32[]{:S(2)}) collective-permute-start(bf16[2272,256]{1,0:T(8,128)(2,1)} %collective-permute-done.22.refs_8_), channel_id=1, source_target_pairs={{0,32},{8,40},{16,48},{24,56},{32,64},{40,72},{48,80},{56,88},{64,... | collective-permute-start | bytes 3489800 | tf_op jit(solution)/shard_map/ppermute | solution.py:522
  172.0 1.7 copy-start.3
  188.2 3.0 %collective-permute-start.27 = (bf16[64,64,128]{2,1,0:T(8,128)(2,1)}, bf16[64,64,128]{2,1,0:T(8,128)(2,1)S(1)}, u32[]{:S(2)}, u32[]{:S(2)}) collective-permute-start(bf16[64,64,128]{2,1,0:T(8,128)(2,1)} %get-tuple-element.22), channel_id=1, source_target_pairs={{0,1},{1,0},{2,3},{3,2},{4,5},{5,4},{6,7},{7,6},{8,9},{9,8},{10,11... | collective-permute-start | bytes 3145736 | tf_op jit(solution)/shard_map/ppermute | solution.py:522
  193.1 18.2 %copy-start.6 = (f32[16,64,128]{2,1,0:T(8,128)S(1)}, f32[16,64,128]{2,1,0:T(8,128)}, u32[]{:S(2)}) copy-start(f32[16,64,128]{2,1,0:T(8,128)} %get-tuple-element.17) | copy-start | bytes 1572868
  193.2 14.7 %collective-permute-start.28 = (bf16[16,64,128]{2,1,0:T(8,128)(2,1)S(1)}, bf16[16,64,128]{2,1,0:T(8,128)(2,1)S(1)}, u32[]{:S(2)}, u32[]{:S(2)}) collective-permute-start(bf16[16,64,128]{2,1,0:T(8,128)(2,1)S(1)} %get-tuple-element.27), channel_id=1, source_target_pairs={{0,6},{1,7},{2,0},{3,1},{4,2},{5,3},{6,4},{7,5},{8,14},{9,15},{10,... | collective-permute-start | bytes 786440 | tf_op jit(solution)/shard_map/ppermute | solution.py:522
  196.4 14.9 %collective-permute-start.29 = (bf16[16,64,128]{2,1,0:T(8,128)(2,1)S(1)}, bf16[16,64,128]{2,1,0:T(8,128)(2,1)S(1)}, u32[]{:S(2)}, u32[]{:S(2)}) collective-permute-start(bf16[16,64,128]{2,1,0:T(8,128)(2,1)S(1)} %get-tuple-element.29), channel_id=1, source_target_pairs={{0,2},{1,3},{2,4},{3,5},{4,6},{5,7},{6,0},{7,1},{8,10},{9,11},{10,... | collective-permute-start | bytes 786440 | tf_op jit(solution)/shard_map/ppermute | solution.py:522
  196.4 14.9 %collective-permute-start.30 = (bf16[16,64,128]{2,1,0:T(8,128)(2,1)S(1)}, bf16[16,64,128]{2,1,0:T(8,128)(2,1)S(1)}, u32[]{:S(2)}, u32[]{:S(2)}) collective-permute-start(bf16[16,64,128]{2,1,0:T(8,128)(2,1)S(1)} %get-tuple-element.28), channel_id=1, source_target_pairs={{0,4},{1,5},{2,6},{3,7},{4,0},{5,1},{6,2},{7,3},{8,12},{9,13},{10,... | collective-permute-start | bytes 786440 | tf_op jit(solution)/shard_map/ppermute | solution.py:522
  (4 other events, 4.7 us)
